TPU v7x, 128 devices: a whole 4x4x4 slice. The times are simulated.
128 devices in a mesh: gx: 8 (over x, core), gy: 4 (over y), gz: 4 (over z).
Axes of the slice: x: 4, y: 4, z: 4, core: 2. Of those that a mesh axis runs over, the one named last changes fastest.
Arguments:
- start_block: float32 [16, 32, 64, 512], P(None, 'gx', 'gy', 'gz')
- basis: bfloat16 [256, 32, 64, 512], P(None, 'gx', 'gy', 'gz')
- trans_x: float32 [32, 64, 512], P('gx', 'gy', 'gz'), may hold values from 0.05 to 1
- trans_y: float32 [32, 64, 512], P('gx', 'gy', 'gz'), may hold values from 0.05 to 1
- trans_z: float32 [32, 64, 512], P('gx', 'gy', 'gz'), may hold values from 0.05 to 1
- pore_volume: float32 [32, 64, 512], P('gx', 'gy', 'gz'), may hold values from 0.5 to 2
- shift_table: float32 [16], replicated, may hold values from 0.5 to 4
- shift_index: int32 [1], replicated, may hold values from 0 to 15
- fault_send: int32 [128, 128, 32], P(('gx', 'gy', 'gz')), may hold values from 0 to 8191
- fault_recv: int32 [128, 128, 32], P(('gx', 'gy', 'gz')), may hold values from 0 to 8191
- fault_trans: float32 [128, 128, 32], P(('gx', 'gy', 'gz')), may hold values from 0.05 to 0.5
- well_cells: int32 [64], replicated, may hold values from 0 to 1048575
Outputs:
- new_block: float32 [16, 32, 64, 512], P(None, 'gx', 'gy', 'gz')
- first_coeffs: float32 [256, 16], replicated
- coeffs: float32 [256, 16], replicated
- well_resp: float32 [64, 16], replicated
Inputs may be any that keep to these rules, and one draw needn't show every extreme that they name: fault_send[d, p, s] is a local cell number on device d; the value of that cell feeds a connection into device p. fault_recv[d, p, s] is a local cell number on device d. `well_cells`: flat cell index, last dimension fastest.
All inputs are finite; a program needn't handle non-finite values.
Results may differ from a plain program's by a relative error of at most 0.0065.
Values sent between devices are 32-bit elements; how exact they have to be, the bound alone decides.
A program may use at most 128 MiB of HBM per device.

v0:
```python
import math

import jax
import jax.numpy as jnp
from jax import lax
from jax.sharding import PartitionSpec as P

TERMS = 8


def from_behind(value, axis, by):
    size = lax.axis_size(axis)
    pairs = [(i, i + by) for i in range(size) if 0 <= i + by < size]
    return lax.ppermute(value, axis, pairs)


def extended(value, sides, width):
    for axis, dim in sides:
        size, length = (lax.axis_size(axis), value.shape[dim])
        up = [(i, (i + 1) % size) for i in range(size - 1)]
        down = [(j, i) for i, j in up]
        last = lax.slice_in_dim(value, length - width, length, axis=dim)
        initial = lax.slice_in_dim(value, 0, width, axis=dim)
        before = lax.ppermute(last, axis, up)
        after = lax.ppermute(initial, axis, down)
        value = jnp.concatenate([before, value, after], axis=dim)
    return value


def local(
    start_block,
    basis,
    trans_x,
    trans_y,
    trans_z,
    pore_volume,
    shift_table,
    shift_index,
    fault_send,
    fault_recv,
    fault_trans,
    well_cells,
):
    columns, size_x, size_y, size_z = start_block.shape
    cells = size_x * size_y * size_z
    count_x = lax.axis_size("gx")
    count_y = lax.axis_size("gy")
    count_z = lax.axis_size("gz")
    index_x = lax.axis_index("gx")
    index_y = lax.axis_index("gy")
    index_z = lax.axis_index("gz")
    full_x = size_x * count_x
    full_y = size_y * count_y
    full_z = size_z * count_z
    shape3 = (size_x, size_y, size_z)
    pos_x = lax.broadcasted_iota(jnp.int32, shape3, 0) + index_x * size_x
    pos_y = lax.broadcasted_iota(jnp.int32, shape3, 1) + index_y * size_y
    pos_z = lax.broadcasted_iota(jnp.int32, shape3, 2) + index_z * size_z
    upper_x = jnp.where(pos_x < full_x - 1, trans_x, 0.0)
    upper_y = jnp.where(pos_y < full_y - 1, trans_y, 0.0)
    upper_z = jnp.where(pos_z < full_z - 1, trans_z, 0.0)
    edge_x = from_behind(upper_x[-1:, :, :], "gx", 1)
    edge_y = from_behind(upper_y[:, -1:, :], "gy", 1)
    edge_z = from_behind(upper_z[:, :, -1:], "gz", 1)
    lower_x = jnp.concatenate([edge_x, upper_x[:-1, :, :]], axis=0)
    lower_y = jnp.concatenate([edge_y, upper_y[:, :-1, :]], axis=1)
    lower_z = jnp.concatenate([edge_z, upper_z[:, :, :-1]], axis=2)
    shift = jnp.sum(
        jnp.where(
            jnp.arange(shift_table.shape[0], dtype=jnp.int32) == shift_index[0], shift_table, 0.0
        )
    )
    send_flat = fault_send[0].reshape(-1)
    recv_flat = fault_recv[0].reshape(-1)
    weight_flat = fault_trans[0].reshape(-1)
    fault_diag = jnp.zeros((cells,), jnp.float32).at[recv_flat].add(weight_flat).reshape(shape3)
    diagonal = (
        upper_x + lower_x + upper_y + lower_y + upper_z + lower_z + shift * pore_volume + fault_diag
    )
    sigma = 1.0 / 0.9
    weight_now = 1.0 / sigma
    solution = jnp.zeros_like(start_block)
    residual = start_block
    direction = residual / diagonal
    for number in range(TERMS):
        solution = solution + direction
        if number < TERMS - 1:
            grown = extended(direction, (("gx", 1), ("gy", 2), ("gz", 3)), 1)
            operate_flat = direction.reshape(columns, cells)
            incoming = lax.all_to_all(
                operate_flat[:, send_flat],
                ("gx", "gy", "gz"),
                split_axis=1,
                concat_axis=1,
                tiled=True,
            )
            beside = upper_x * grown[:, 2:, 1:-1, 1:-1] + lower_x * grown[:, :-2, 1:-1, 1:-1]
            beside = (
                beside + upper_y * grown[:, 1:-1, 2:, 1:-1] + lower_y * grown[:, 1:-1, :-2, 1:-1]
            )
            beside = (
                beside + upper_z * grown[:, 1:-1, 1:-1, 2:] + lower_z * grown[:, 1:-1, 1:-1, :-2]
            )
            remote = (
                jnp.zeros((columns, cells), jnp.float32)
                .at[:, recv_flat]
                .add(weight_flat * incoming)
            )
            residual = residual - (diagonal * direction - beside - remote.reshape(direction.shape))
            weight_new = 1.0 / (2.0 * sigma - weight_now)
            direction = weight_new * weight_now * direction + 2.0 * weight_new / 0.9 * (
                residual / diagonal
            )
            weight_now = weight_new
    plane = full_y * full_z
    well_x = well_cells // plane
    well_y = well_cells // full_z % full_y
    well_z = well_cells % full_z
    owned = (
        (well_x // size_x == index_x)
        & (well_y // size_y == index_y)
        & (well_z // size_z == index_z)
    )
    local_cell = (well_x % size_x * size_y + well_y % size_y) * size_z + well_z % size_z
    flat_basis = basis.reshape(basis.shape[0], cells)
    flat_x = solution.reshape(columns, cells)
    first_term = jnp.dot(
        flat_basis, flat_x.astype(jnp.bfloat16).T, preferred_element_type=jnp.float32
    )
    first_coeffs = lax.psum(first_term, ("gx", "gy", "gz"))
    first_rest = flat_x - jnp.dot(
        first_coeffs.astype(jnp.bfloat16).T, flat_basis, preferred_element_type=jnp.float32
    )
    second_term = jnp.dot(
        flat_basis, first_rest.astype(jnp.bfloat16).T, preferred_element_type=jnp.float32
    )
    second_coeffs = lax.psum(second_term, ("gx", "gy", "gz"))
    rest = first_rest - jnp.dot(
        second_coeffs.astype(jnp.bfloat16).T, flat_basis, preferred_element_type=jnp.float32
    )
    gram_term = jnp.dot(rest, rest.T, precision=lax.Precision.HIGHEST)
    gram, wells_value = lax.psum(
        (gram_term, jnp.where(owned[None, :], rest[:, local_cell], 0.0)), ("gx", "gy", "gz")
    )
    lower = jnp.linalg.cholesky(gram)
    scale = math.sqrt(full_x * full_y * full_z)
    new_flat = lax.linalg.triangular_solve(lower, rest, left_side=True, lower=True) * scale
    well_resp = (
        lax.linalg.triangular_solve(lower, wells_value, left_side=True, lower=True) * scale
    ).T
    return (
        new_flat.reshape(start_block.shape),
        first_coeffs,
        first_coeffs + second_coeffs,
        well_resp,
    )


def solution(mesh):
    in_specs = (
        P(None, "gx", "gy", "gz"),
        P(None, "gx", "gy", "gz"),
        P("gx", "gy", "gz"),
        P("gx", "gy", "gz"),
        P("gx", "gy", "gz"),
        P("gx", "gy", "gz"),
        P(),
        P(),
        P(("gx", "gy", "gz"), None, None),
        P(("gx", "gy", "gz"), None, None),
        P(("gx", "gy", "gz"), None, None),
        P(),
    )
    out_specs = (P(None, "gx", "gy", "gz"), P(), P(), P())
    return jax.shard_map(local, mesh=mesh, in_specs=in_specs, out_specs=out_specs, check_vma=False)
```

profile of v0, /device:TPU:1, one launch (start us, length us, event | category | flops | bytes accessed | tf_op | source)
XLA Modules:
  0.0 1015.0 jit_solution(15570318955301733830)
XLA Ops:
  1.6 4.5 collective-permute-start
  19.2 21.9 %scatter_custom_fusion = f32[8192]{0:T(1024)S(1)} fusion(s32[4096]{0:T(1024)S(1)} %bitcast.158, f32[4096]{0:T(1024)S(1)} %reshape.239, f32[]{:T(128)} %constant.173.clone.1), kind=kCustom, calls=%fused_computation.323 | custom fusion | flops 4096 | bytes 32772 | tf_op jit(solution)/shard_map/scatter-add | solution.py:76
  45.4 3.6 collective-permute-start.4
  52.3 4.0 collective-permute-start.6
  59.0 16.4 %gather_fusion = f32[4096,16]{1,0:T(8,128)} fusion(f32[16,8192]{0,1:T(8,128)} %bitcast.125, s32[4096]{0:T(1024)S(1)} %broadcast_clamp_fusion), kind=kCustom, calls=%fused_computation | custom fusion | bytes 540672 | tf_op jit(solution)/shard_map/gather | solution.py:91
  78.8 11.2 %all-to-all-start = ((f32[128,1,512]{2,1,0:T(1,128)}), f32[128,1,512]{2,1,0:T(1,128)S(1)}, u32[]{:S(2)}, u32[]{:S(2)}) async-start(f32[128,1,512]{2,1,0:T(1,128)} %reshape.317), calls=%async_computation | async-start | bytes 524288 | tf_op jit(solution)/shard_map/all_to_all | solution.py:90
  113.2 25.0 %scatter_custom_fusion.1 = f32[16,8192]{0,1:T(8,128)} fusion(s32[4096]{0:T(1024)} %bitcast.159, f32[4096,16]{1,0:T(8,128)} %copy.299, f32[]{:T(128)} %constant.173.clone.1), kind=kCustom, calls=%fused_computation.40 | custom fusion | flops 65536 | bytes 524800 | tf_op jit(solution)/shard_map/scatter-add | solution.py:107
  138.2 3.6 copy.300
  144.7 3.6 collective-permute-start.9
  154.6 4.0 collective-permute-start.12
  161.3 16.4 %gather_fusion.1 = f32[4096,16]{1,0:T(8,128)} fusion(f32[16,8192]{0,1:T(8,128)} %bitcast.126, s32[4096]{0:T(1024)S(1)} %broadcast_clamp_fusion), kind=kCustom, calls=%fused_computation.1 | custom fusion | bytes 540672 | tf_op jit(solution)/shard_map/gather | solution.py:91
  181.0 11.4 %all-to-all-start.1 = ((f32[128,1,512]{2,1,0:T(1,128)}), f32[128,1,512]{2,1,0:T(1,128)}, u32[]{:S(2)}, u32[]{:S(2)}) async-start(f32[128,1,512]{2,1,0:T(1,128)} %reshape.319), calls=%async_computation.1 | async-start | bytes 524288 | tf_op jit(solution)/shard_map/all_to_all | solution.py:90
  216.0 24.8 %scatter_custom_fusion.2 = f32[16,8192]{0,1:T(8,128)} fusion(s32[4096]{0:T(1024)} %bitcast.160, f32[4096,16]{1,0:T(8,128)} %copy.314, f32[]{:T(128)} %constant.173.clone.1), kind=kCustom, calls=%fused_computation.38 | custom fusion | flops 65536 | bytes 524800 | tf_op jit(solution)/shard_map/scatter-add | solution.py:107
  240.9 3.5 copy.315
  247.3 3.7 collective-permute-start.15
  257.6 4.0 collective-permute-start.18
  264.2 16.4 %gather_fusion.2 = f32[4096,16]{1,0:T(8,128)} fusion(f32[16,8192]{0,1:T(8,128)} %bitcast.127, s32[4096]{0:T(1024)S(1)} %broadcast_clamp_fusion), kind=kCustom, calls=%fused_computation.2 | custom fusion | bytes 540672 | tf_op jit(solution)/shard_map/gather | solution.py:91
  284.0 11.4 %all-to-all-start.2 = ((f32[128,1,512]{2,1,0:T(1,128)}), f32[128,1,512]{2,1,0:T(1,128)}, u32[]{:S(2)}, u32[]{:S(2)}) async-start(f32[128,1,512]{2,1,0:T(1,128)} %reshape.321), calls=%async_computation.2 | async-start | bytes 524288 | tf_op jit(solution)/shard_map/all_to_all | solution.py:90
  319.0 24.8 %scatter_custom_fusion.3 = f32[16,8192]{0,1:T(8,128)} fusion(s32[4096]{0:T(1024)} %bitcast.161, f32[4096,16]{1,0:T(8,128)} %copy.329, f32[]{:T(128)} %constant.173.clone.1), kind=kCustom, calls=%fused_computation.36 | custom fusion | flops 65536 | bytes 524800 | tf_op jit(solution)/shard_map/scatter-add | solution.py:107
  349.8 3.7 collective-permute-start.21
  359.9 4.0 collective-permute-start.24
  366.5 16.4 %gather_fusion.3 = f32[4096,16]{1,0:T(8,128)} fusion(f32[16,8192]{0,1:T(8,128)} %bitcast.128, s32[4096]{0:T(1024)S(1)} %broadcast_clamp_fusion), kind=kCustom, calls=%fused_computation.3 | custom fusion | bytes 540672 | tf_op jit(solution)/shard_map/gather | solution.py:91
  386.3 11.4 %all-to-all-start.3 = ((f32[128,1,512]{2,1,0:T(1,128)}), f32[128,1,512]{2,1,0:T(1,128)}, u32[]{:S(2)}, u32[]{:S(2)}) async-start(f32[128,1,512]{2,1,0:T(1,128)} %reshape.323), calls=%async_computation.3 | async-start | bytes 524288 | tf_op jit(solution)/shard_map/all_to_all | solution.py:90
  401.4 4.0 collective-permute-start.26
  423.3 24.8 %scatter_custom_fusion.4 = f32[16,8192]{0,1:T(8,128)} fusion(s32[4096]{0:T(1024)} %bitcast.162, f32[4096,16]{1,0:T(8,128)} %copy.344, f32[]{:T(128)} %constant.173.clone.1), kind=kCustom, calls=%fused_computation.34 | custom fusion | flops 65536 | bytes 524800 | tf_op jit(solution)/shard_map/scatter-add | solution.py:107
  454.9 3.7 collective-permute-start.27
  466.1 4.6 collective-permute-start.30
  473.4 16.4 %gather_fusion.4 = f32[4096,16]{1,0:T(8,128)} fusion(f32[16,8192]{0,1:T(8,128)} %bitcast.129, s32[4096]{0:T(1024)S(1)} %broadcast_clamp_fusion), kind=kCustom, calls=%fused_computation.4 | custom fusion | bytes 540672 | tf_op jit(solution)/shard_map/gather | solution.py:91
  493.1 10.8 %all-to-all-start.4 = ((f32[128,1,512]{2,1,0:T(1,128)}), f32[128,1,512]{2,1,0:T(1,128)}, u32[]{:S(2)}, u32[]{:S(2)}) async-start(f32[128,1,512]{2,1,0:T(1,128)} %reshape.325), calls=%async_computation.4 | async-start | bytes 524288 | tf_op jit(solution)/shard_map/all_to_all | solution.py:90
  511.4 4.1 collective-permute-start.32
  532.9 24.8 %scatter_custom_fusion.5 = f32[16,8192]{0,1:T(8,128)} fusion(s32[4096]{0:T(1024)} %bitcast.163, f32[4096,16]{1,0:T(8,128)} %copy.359, f32[]{:T(128)} %constant.173.clone.1), kind=kCustom, calls=%fused_computation.32 | custom fusion | flops 65536 | bytes 524800 | tf_op jit(solution)/shard_map/scatter-add | solution.py:107
  563.9 3.7 collective-permute-start.33
  575.1 4.6 collective-permute-start.36
  582.4 16.4 %gather_fusion.5 = f32[4096,16]{1,0:T(8,128)} fusion(f32[16,8192]{0,1:T(8,128)} %bitcast.130, s32[4096]{0:T(1024)S(1)} %broadcast_clamp_fusion), kind=kCustom, calls=%fused_computation.5 | custom fusion | bytes 540672 | tf_op jit(solution)/shard_map/gather | solution.py:91
  604.3 9.8 all-to-all-start.5
  639.8 24.8 %scatter_custom_fusion.6 = f32[16,8192]{0,1:T(8,128)} fusion(s32[4096]{0:T(1024)} %bitcast.164, f32[4096,16]{1,0:T(8,128)} %copy.374, f32[]{:T(128)} %constant.173.clone.1), kind=kCustom, calls=%fused_computation.30 | custom fusion | flops 65536 | bytes 524800 | tf_op jit(solution)/shard_map/scatter-add | solution.py:107
  671.6 3.7 collective-permute-start.39
  683.5 4.6 collective-permute-start.42
  690.8 16.4 %gather_fusion.6 = f32[4096,16]{1,0:T(8,128)} fusion(f32[16,8192]{0,1:T(8,128)} %bitcast.124, s32[4096]{0:T(1024)S(1)} %broadcast_clamp_fusion), kind=kCustom, calls=%fused_computation.6 | custom fusion | bytes 540672 | tf_op jit(solution)/shard_map/gather | solution.py:91
  712.8 11.4 %all-to-all-start.6 = ((f32[128,1,512]{2,1,0:T(1,128)}), f32[128,1,512]{2,1,0:T(1,128)}, u32[]{:S(2)}, u32[]{:S(2)}) async-start(f32[128,1,512]{2,1,0:T(1,128)} %reshape.329), calls=%async_computation.6 | async-start | bytes 524288 | tf_op jit(solution)/shard_map/all_to_all | solution.py:90
  732.0 4.0 collective-permute-start.44
  761.0 24.8 %scatter_custom_fusion.7 = f32[16,8192]{0,1:T(8,128)} fusion(s32[4096]{0:T(1024)} %bitcast.165, f32[4096,16]{1,0:T(8,128)} %copy.389, f32[]{:T(128)} %constant.173.clone.1), kind=kCustom, calls=%fused_computation.28 | custom fusion | flops 65536 | bytes 524800 | tf_op jit(solution)/shard_map/scatter-add | solution.py:107
  789.4 3.9 fusion.144
  795.7 67.1 %psum.28 = f32[256,16]{0,1:T(8,128)S(1)} all-reduce(f32[256,16]{0,1:T(8,128)S(1)} %fusion.24), channel_id=1, replica_groups=mesh['gx'=8,'gy'=4,'gz'=4] {'gx','gy','gz'}, use_global_device_ids=true, to_apply=%region_9.10 | all-reduce | flops 4096 | bytes 32768 | tf_op jit(solution)/shard_map/psum | solution.py:130
  862.8 4.9 convolution_subtract_fusion.1
  870.0 62.8 %psum.29 = f32[256,16]{0,1:T(8,128)S(1)} all-reduce(f32[256,16]{0,1:T(8,128)S(1)} %fusion.27), channel_id=1, replica_groups=mesh['gx'=8,'gy'=4,'gz'=4] {'gx','gy','gz'}, use_global_device_ids=true, to_apply=%region_10.11 | all-reduce | flops 4096 | bytes 32768 | tf_op jit(solution)/shard_map/psum | solution.py:137
  932.8 4.5 convolution_subtract_fusion
  944.2 64.1 %all-reduce = (f32[16,16]{0,1:T(8,128)S(1)}, f32[16,64]{0,1:T(8,128)S(1)}) all-reduce(f32[16,16]{0,1:T(8,128)S(1)} %fusion.165, f32[16,64]{0,1:T(8,128)S(1)} %select_bitcast_fusion), channel_id=1, replica_groups=mesh['gx'=8,'gy'=4,'gz'=4] {'gx','gy','gz'}, use_global_device_ids=true, to_apply=%region_11.12 | all-reduce | flops 1280 | bytes 10240 | tf_op jit(solution)/shard_map/psum | solution.py:142
  (362 shorter events, 337.3 us)
Async XLA Ops:
  1.6 39.6 %collective-permute-start = (f32[1,16,128]{2,1,0:T(8,128)S(1)}, f32[1,16,128]{2,1,0:T(8,128)S(1)}, u32[]{:S(2)}, u32[]{:S(2)}) collective-permute-start(f32[1,16,128]{2,1,0:T(8,128)S(1)} %slice.432), channel_id=1, source_target_pairs={{0,16},{16,32},{32,48},{48,64},{64,80},{80,96},{96,112},{1,17},{17... | collective-permute-start | bytes 24584 | tf_op jit(solution)/shard_map/ppermute | solution.py:14
  6.9 34.3 %collective-permute-start.1 = (f32[4,1,128]{2,1,0:T(1,128)S(1)}, f32[4,1,128]{2,1,0:T(1,128)S(1)}, u32[]{:S(2)}, u32[]{:S(2)}) collective-permute-start(f32[4,1,128]{2,1,0:T(1,128)S(1)} %slice.434), channel_id=1, source_target_pairs={{0,4},{4,8},{8,12},{1,5},{5,9},{9,13},{2,6},{6,10},{10,14},{3,7},{... | collective-permute-start | bytes 6152 | tf_op jit(solution)/shard_map/ppermute | solution.py:14
  11.0 30.2 %collective-permute-start.2 = (f32[4,16,1]{2,1,0:T(8,128)S(1)}, f32[4,16,1]{2,1,0:T(8,128)S(1)}, u32[]{:S(2)}, u32[]{:S(2)}) collective-permute-start(f32[4,16,1]{2,1,0:T(8,128)S(1)} %slice.436), channel_id=1, source_target_pairs={{0,1},{1,2},{2,3},{4,5},{5,6},{6,7},{8,9},{9,10},{10,11},{12,13},{... | collective-permute-start | bytes 776 | tf_op jit(solution)/shard_map/ppermute | solution.py:14
  43.4 6.3 collective-permute-start.3
  45.4 5.6 collective-permute-start.4
  51.0 38.9 %collective-permute-start.5 = (f32[16,6,1,128]{3,0,2,1:T(8,128)S(1)}, f32[16,6,1,128]{3,0,2,1:T(8,128)S(1)}, u32[]{:S(2)}, u32[]{:S(2)}) collective-permute-start(f32[16,6,1,128]{3,0,2,1:T(8,128)S(1)} %copy.398), channel_id=1, source_target_pairs={{4,0},{8,4},{12,8},{5,1},{9,5},{13,9},{6,2},{10,6},{14,10},{7,3},{... | collective-permute-start | bytes 147464 | tf_op jit(solution)/shard_map/ppermute | solution.py:25
  52.3 37.7 %collective-permute-start.6 = (f32[16,6,1,128]{3,0,2,1:T(8,128)S(1)}, f32[16,6,1,128]{3,0,2,1:T(8,128)S(1)}, u32[]{:S(2)}, u32[]{:S(2)}) collective-permute-start(f32[16,6,1,128]{3,0,2,1:T(8,128)S(1)} %copy.399), channel_id=1, source_target_pairs={{0,4},{4,8},{8,12},{1,5},{5,9},{9,13},{2,6},{6,10},{10,14},{3,7},{... | collective-permute-start | bytes 147464 | tf_op jit(solution)/shard_map/ppermute | solution.py:24
  78.8 23.4 %all-to-all-start = ((f32[128,1,512]{2,1,0:T(1,128)}), f32[128,1,512]{2,1,0:T(1,128)S(1)}, u32[]{:S(2)}, u32[]{:S(2)}) async-start(f32[128,1,512]{2,1,0:T(1,128)} %reshape.317), calls=%async_computation | async-start | bytes 524288 | tf_op jit(solution)/shard_map/all_to_all | solution.py:90
  92.5 5.3 collective-permute-start.8
  96.5 5.0 collective-permute-start.7
  144.7 7.3 collective-permute-start.9
  148.3 4.9 collective-permute-start.10
  153.3 39.2 %collective-permute-start.11 = (f32[16,6,1,128]{3,0,2,1:T(8,128)S(1)}, f32[16,6,1,128]{3,0,2,1:T(8,128)S(1)}, u32[]{:S(2)}, u32[]{:S(2)}) collective-permute-start(f32[16,6,1,128]{3,0,2,1:T(8,128)S(1)} %copy.400), channel_id=1, source_target_pairs={{4,0},{8,4},{12,8},{5,1},{9,5},{13,9},{6,2},{10,6},{14,10},{7,3},{... | collective-permute-start | bytes 147464 | tf_op jit(solution)/shard_map/ppermute | solution.py:25
  154.6 37.9 %collective-permute-start.12 = (f32[16,6,1,128]{3,0,2,1:T(8,128)S(1)}, f32[16,6,1,128]{3,0,2,1:T(8,128)S(1)}, u32[]{:S(2)}, u32[]{:S(2)}) collective-permute-start(f32[16,6,1,128]{3,0,2,1:T(8,128)S(1)} %copy.401), channel_id=1, source_target_pairs={{0,4},{4,8},{8,12},{1,5},{5,9},{9,13},{2,6},{6,10},{10,14},{3,7},{... | collective-permute-start | bytes 147464 | tf_op jit(solution)/shard_map/ppermute | solution.py:24
  181.0 23.5 %all-to-all-start.1 = ((f32[128,1,512]{2,1,0:T(1,128)}), f32[128,1,512]{2,1,0:T(1,128)}, u32[]{:S(2)}, u32[]{:S(2)}) async-start(f32[128,1,512]{2,1,0:T(1,128)} %reshape.319), calls=%async_computation.1 | async-start | bytes 524288 | tf_op jit(solution)/shard_map/all_to_all | solution.py:90
  195.0 5.3 collective-permute-start.14
  247.3 7.5 collective-permute-start.15
  256.1 39.4 %collective-permute-start.17 = (f32[16,6,1,128]{3,0,2,1:T(8,128)S(1)}, f32[16,6,1,128]{3,0,2,1:T(8,128)S(1)}, u32[]{:S(2)}, u32[]{:S(2)}) collective-permute-start(f32[16,6,1,128]{3,0,2,1:T(8,128)S(1)} %copy.402), channel_id=1, source_target_pairs={{4,0},{8,4},{12,8},{5,1},{9,5},{13,9},{6,2},{10,6},{14,10},{7,3},{... | collective-permute-start | bytes 147464 | tf_op jit(solution)/shard_map/ppermute | solution.py:25
  257.6 37.9 %collective-permute-start.18 = (f32[16,6,1,128]{3,0,2,1:T(8,128)S(1)}, f32[16,6,1,128]{3,0,2,1:T(8,128)S(1)}, u32[]{:S(2)}, u32[]{:S(2)}) collective-permute-start(f32[16,6,1,128]{3,0,2,1:T(8,128)S(1)} %copy.403), channel_id=1, source_target_pairs={{0,4},{4,8},{8,12},{1,5},{5,9},{9,13},{2,6},{6,10},{10,14},{3,7},{... | collective-permute-start | bytes 147464 | tf_op jit(solution)/shard_map/ppermute | solution.py:24
  284.0 25.2 %all-to-all-start.2 = ((f32[128,1,512]{2,1,0:T(1,128)}), f32[128,1,512]{2,1,0:T(1,128)}, u32[]{:S(2)}, u32[]{:S(2)}) async-start(f32[128,1,512]{2,1,0:T(1,128)} %reshape.321), calls=%async_computation.2 | async-start | bytes 524288 | tf_op jit(solution)/shard_map/all_to_all | solution.py:90
  298.6 5.3 collective-permute-start.20
  349.8 7.5 collective-permute-start.21
  353.5 4.9 collective-permute-start.22
  358.6 39.2 %collective-permute-start.23 = (f32[16,6,1,128]{3,0,2,1:T(8,128)S(1)}, f32[16,6,1,128]{3,0,2,1:T(8,128)S(1)}, u32[]{:S(2)}, u32[]{:S(2)}) collective-permute-start(f32[16,6,1,128]{3,0,2,1:T(8,128)S(1)} %copy.404), channel_id=1, source_target_pairs={{4,0},{8,4},{12,8},{5,1},{9,5},{13,9},{6,2},{10,6},{14,10},{7,3},{... | collective-permute-start | bytes 147464 | tf_op jit(solution)/shard_map/ppermute | solution.py:25
  359.9 37.9 %collective-permute-start.24 = (f32[16,6,1,128]{3,0,2,1:T(8,128)S(1)}, f32[16,6,1,128]{3,0,2,1:T(8,128)S(1)}, u32[]{:S(2)}, u32[]{:S(2)}) collective-permute-start(f32[16,6,1,128]{3,0,2,1:T(8,128)S(1)} %copy.405), channel_id=1, source_target_pairs={{0,4},{4,8},{8,12},{1,5},{5,9},{9,13},{2,6},{6,10},{10,14},{3,7},{... | collective-permute-start | bytes 147464 | tf_op jit(solution)/shard_map/ppermute | solution.py:24
  386.3 27.2 %all-to-all-start.3 = ((f32[128,1,512]{2,1,0:T(1,128)}), f32[128,1,512]{2,1,0:T(1,128)}, u32[]{:S(2)}, u32[]{:S(2)}) async-start(f32[128,1,512]{2,1,0:T(1,128)} %reshape.323), calls=%async_computation.3 | async-start | bytes 524288 | tf_op jit(solution)/shard_map/all_to_all | solution.py:90
  401.4 6.5 collective-permute-start.26
  406.7 5.0 collective-permute-start.25
  454.9 7.5 collective-permute-start.27
  458.6 4.9 collective-permute-start.28
  464.2 39.8 %collective-permute-start.29 = (f32[16,6,1,128]{3,0,2,1:T(8,128)}, f32[16,6,1,128]{3,0,2,1:T(8,128)}, u32[]{:S(2)}, u32[]{:S(2)}) collective-permute-start(f32[16,6,1,128]{3,0,2,1:T(8,128)} %copy.406), channel_id=1, source_target_pairs={{4,0},{8,4},{12,8},{5,1},{9,5},{13,9},{6,2},{10,6},{14,10},{7,3},{... | collective-permute-start | bytes 147464 | tf_op jit(solution)/shard_map/ppermute | solution.py:25
  466.1 38.7 %collective-permute-start.30 = (f32[16,6,1,128]{3,0,2,1:T(8,128)}, f32[16,6,1,128]{3,0,2,1:T(8,128)}, u32[]{:S(2)}, u32[]{:S(2)}) collective-permute-start(f32[16,6,1,128]{3,0,2,1:T(8,128)} %copy.407), channel_id=1, source_target_pairs={{0,4},{4,8},{8,12},{1,5},{5,9},{9,13},{2,6},{6,10},{10,14},{3,7},{... | collective-permute-start | bytes 147464 | tf_op jit(solution)/shard_map/ppermute | solution.py:24
  493.1 30.5 %all-to-all-start.4 = ((f32[128,1,512]{2,1,0:T(1,128)}), f32[128,1,512]{2,1,0:T(1,128)}, u32[]{:S(2)}, u32[]{:S(2)}) async-start(f32[128,1,512]{2,1,0:T(1,128)} %reshape.325), calls=%async_computation.4 | async-start | bytes 524288 | tf_op jit(solution)/shard_map/all_to_all | solution.py:90
  511.4 6.7 collective-permute-start.32
  516.8 5.0 collective-permute-start.31
  563.9 7.5 collective-permute-start.33
  567.6 4.9 collective-permute-start.34
  573.2 40.9 %collective-permute-start.35 = (f32[16,6,1,128]{3,0,2,1:T(8,128)}, f32[16,6,1,128]{3,0,2,1:T(8,128)S(1)}, u32[]{:S(2)}, u32[]{:S(2)}) collective-permute-start(f32[16,6,1,128]{3,0,2,1:T(8,128)} %copy.408), channel_id=1, source_target_pairs={{4,0},{8,4},{12,8},{5,1},{9,5},{13,9},{6,2},{10,6},{14,10},{7,3},{... | collective-permute-start | bytes 147464 | tf_op jit(solution)/shard_map/ppermute | solution.py:25
  575.1 39.1 %collective-permute-start.36 = (f32[16,6,1,128]{3,0,2,1:T(8,128)}, f32[16,6,1,128]{3,0,2,1:T(8,128)}, u32[]{:S(2)}, u32[]{:S(2)}) collective-permute-start(f32[16,6,1,128]{3,0,2,1:T(8,128)} %copy.409), channel_id=1, source_target_pairs={{0,4},{4,8},{8,12},{1,5},{5,9},{9,13},{2,6},{6,10},{10,14},{3,7},{... | collective-permute-start | bytes 147464 | tf_op jit(solution)/shard_map/ppermute | solution.py:24
  604.3 26.6 %all-to-all-start.5 = ((f32[128,1,512]{2,1,0:T(1,128)}), f32[128,1,512]{2,1,0:T(1,128)S(1)}, u32[]{:S(2)}, u32[]{:S(2)}) async-start(f32[128,1,512]{2,1,0:T(1,128)} %reshape.327), calls=%async_computation.5 | async-start | bytes 524288 | tf_op jit(solution)/shard_map/all_to_all | solution.py:90
  619.0 6.8 collective-permute-start.38
  671.6 7.5 collective-permute-start.39
  675.3 4.9 collective-permute-start.40
  681.6 42.6 %collective-permute-start.41 = (f32[16,6,1,128]{3,0,2,1:T(8,128)}, f32[16,6,1,128]{3,0,2,1:T(8,128)}, u32[]{:S(2)}, u32[]{:S(2)}) collective-permute-start(f32[16,6,1,128]{3,0,2,1:T(8,128)} %copy.410), channel_id=1, source_target_pairs={{4,0},{8,4},{12,8},{5,1},{9,5},{13,9},{6,2},{10,6},{14,10},{7,3},{... | collective-permute-start | bytes 147464 | tf_op jit(solution)/shard_map/ppermute | solution.py:25
  683.5 41.6 %collective-permute-start.42 = (f32[16,6,1,128]{3,0,2,1:T(8,128)}, f32[16,6,1,128]{3,0,2,1:T(8,128)}, u32[]{:S(2)}, u32[]{:S(2)}) collective-permute-start(f32[16,6,1,128]{3,0,2,1:T(8,128)} %copy.411), channel_id=1, source_target_pairs={{0,4},{4,8},{8,12},{1,5},{5,9},{9,13},{2,6},{6,10},{10,14},{3,7},{... | collective-permute-start | bytes 147464 | tf_op jit(solution)/shard_map/ppermute | solution.py:24
  712.8 33.5 %all-to-all-start.6 = ((f32[128,1,512]{2,1,0:T(1,128)}), f32[128,1,512]{2,1,0:T(1,128)}, u32[]{:S(2)}, u32[]{:S(2)}) async-start(f32[128,1,512]{2,1,0:T(1,128)} %reshape.329), calls=%async_computation.6 | async-start | bytes 524288 | tf_op jit(solution)/shard_map/all_to_all | solution.py:90
  732.0 8.2 collective-permute-start.44
  738.5 5.1 collective-permute-start.43
  (45 other events, 729.7 us)
where the time goes:
time: 1030 us; the launch traced here: 1010 us
  local copies, waits for them, and re-layouts  314 us (30%)
  other arithmetic  251 us (24%)
  starting transfers between devices  209 us (20%)
  blocking collectives  194 us (19%)
  waiting for transfers between devices  28 us (3%)
  matrix products  16.4 us (2%)
    scatter-add x7, other arithmetic, local(): remote = jnp.zeros((columns, cells), jnp.float32).at[:, recv_flat].add(we...  174 us
    gather x7, local copies, waits for them, and re-layouts, local(): operate_flat[:, send_flat]  115 us
    all_to_all x7, starting transfers between devices, local(): lax.all_to_all(operate_flat[:, send_flat], ('gx', 'gy', 'gz'), split_axis...  77.5 us
    ppermute x21, starting transfers between devices, extended(): before = lax.ppermute(last, axis, up)  77 us
    psum x1, blocking collectives, local(): first_coeffs = lax.psum(first_term, ('gx', 'gy', 'gz'))  67.1 us
    psum x1, blocking collectives, local(): lax.psum((gram_term, jnp.where(owned[None, :], rest[:, local_cell], 0.0))...  64.1 us
    psum x1, blocking collectives, local(): second_coeffs = lax.psum(second_term, ('gx', 'gy', 'gz'))  62.8 us
    all_to_all x22, local copies, waits for them, and re-layouts, local(): lax.all_to_all(operate_flat[:, send_flat], ('gx', 'gy', 'gz'), split_axis...  47.2 us
  transfers between devices with their start and end apart: 52, of which 21 were waited for; matrix products, arithmetic and copies ran while one was open for 24% of the time, Pallas kernels for 0%

commit v1 on v0

v1 whole, which is shorter than its diff:
```python
import functools
import math

import jax
import jax.numpy as jnp
from jax import lax
from jax.experimental import pallas as pl
from jax.experimental.pallas import tpu as pltpu
from jax.sharding import PartitionSpec as P

TERMS = 8
MESH = pl.DeviceIdType.MESH
F32 = jnp.float32
BF16 = jnp.bfloat16
SIGMA = 1.0 / 0.9


def weights():
    now = 1.0 / SIGMA
    table = []
    for _ in range(TERMS - 1):
        new = 1.0 / (2.0 * SIGMA - now)
        table.append((new * now, 2.0 * new / 0.9))
        now = new
    return table


def zigzag(i, half):
    return half + ((i + 1) // 2) * (1 - 2 * (i % 2))


def offsets(slot):
    return (zigzag(slot // 16, 4), zigzag(slot // 4 % 4, 2), zigzag(slot % 4, 2))


def peer(slot, place, sign):
    (ox, oy, oz), (ax, ay, az) = offsets(slot), place
    return ((ax + sign * ox + 8) % 8, (ay + sign * oy + 4) % 4, (az + sign * oz + 4) % 4)


def number(coords):
    return coords[0] * 16 + coords[1] * 4 + coords[2]


def lanes(shape):
    return lax.broadcasted_iota(jnp.int32, shape, len(shape) - 1)


def half_swap(first, second):
    low = lanes(first.shape) < 64
    return (
        jnp.where(low, first, pltpu.roll(second, 64, 1)),
        jnp.where(low, pltpu.roll(first, 64, 1), second),
    )


def quarter_swap(value):
    upper = lax.broadcasted_iota(jnp.int32, value.shape, 0) // 4
    odd = lanes(value.shape) // 32 % 2
    moved = jnp.where(upper == 0, pltpu.roll(value, 96, 1), pltpu.roll(value, 32, 1))
    return jnp.where(upper == odd, value, pltpu.roll(moved, 4, 0))


def solve_kernel(
    start_ref, tx_ref, ty_ref, tz_ref, pv_ref, table_ref, index_ref, fs_ref, fr_ref, ft_ref,
    out_ref,
    dpad, dbf, res, acc, amat, ohs, ohr, his, hir, wr, send, recv, zsend, zrecv, coef, edge,
    rows, tsend, trecv,
    ssem, rsem, hssem, hrsem, tssem, trsem,
):
    place = (lax.axis_index("gx"), lax.axis_index("gy"), lax.axis_index("gz"))
    ax, ay, az = place
    up_x, down_x = ((ax + 1) % 8, ay, az), ((ax + 7) % 8, ay, az)
    up_y, down_y = (ax, (ay + 1) % 4, az), (ax, (ay + 3) % 4, az)
    up_z, down_z = (ax, ay, (az + 1) % 4), (ax, ay, (az + 3) % 4)
    barrier = pltpu.get_barrier_semaphore()

    def greet(slot, carry):
        pl.semaphore_signal(barrier, inc=1, device_id=peer(slot, place, 1), device_id_type=MESH)
        return carry

    lax.fori_loop(0, 127, greet, 0)

    def copy(src, dst, ss, rs, where):
        return pltpu.make_async_remote_copy(
            src_ref=src, dst_ref=dst, send_sem=ss, recv_sem=rs, device_id=where, device_id_type=MESH
        )

    def reorder(slot, carry):
        to = number(peer(slot, place, 1))
        source = number(peer(slot, place, -1))
        rows[0, pl.ds(slot, 1), 0:32] = fs_ref[pl.ds(to, 1), :]
        rows[1, pl.ds(slot, 1), 0:32] = fr_ref[pl.ds(source, 1), :]
        return carry

    lax.fori_loop(0, 128, reorder, 0)

    def reorder_weights(slot, carry):
        source = number(peer(slot, place, -1))
        wr[0, pl.ds(slot, 1), 0:32] = ft_ref[pl.ds(source, 1), :]
        return carry

    lax.fori_loop(0, 128, reorder_weights, 0)

    def flat(ref, which, half):
        lane = lanes((16, 128))
        pieces = [ref[which, pl.ds(half * 4 + q, 16, stride=8), :] for q in range(4)]
        total = pieces[0]
        for q in range(1, 4):
            total = jnp.where(lane // 32 == q, pltpu.roll(pieces[q], 32 * q, 1), total)
        return total

    column = lax.broadcasted_iota(jnp.int32, (256, 128), 0)
    for half in range(2):
        send_cells = flat(rows, 0, half)
        recv_cells = flat(rows, 1, half)
        recv_weight = flat(wr, 0, half)
        part = slice(half * 128, half * 128 + 128)
        for j in range(16):
            cell = send_cells[j : j + 1]
            his[j, :, part] = jnp.broadcast_to(cell // 256, (8, 128))
            ohs[j, :, part] = jnp.where(column == cell % 256, 1.0, 0.0).astype(BF16)
            cell = recv_cells[j : j + 1]
            hir[j, :, part] = jnp.broadcast_to((cell // 256).astype(F32), (16, 128)).astype(BF16)
            ohr[j, :, part] = jnp.where(column == cell % 256, 1.0, 0.0).astype(BF16)
            edge[j, :, part] = jnp.broadcast_to(recv_weight[j : j + 1], (8, 128))
    lane = lanes((1, 128))
    line = lane % 64
    first = (line % 2) * 128
    near, far = jnp.where(lane < 64, 127, 0), jnp.where(lane < 64, 0, 127)
    his[16, :, 0:128] = jnp.broadcast_to(line // 2, (8, 128))
    hir[16, :, 0:128] = jnp.broadcast_to((line // 2).astype(F32), (16, 128)).astype(BF16)
    ohs[16, :, 0:128] = jnp.where(column == first + near, 1.0, 0.0).astype(BF16)
    ohr[16, :, 0:128] = jnp.where(column == first + far, 1.0, 0.0).astype(BF16)

    for x in range(4):
        tsend[x : x + 1] = ty_ref[x * 16 + 15 : x * 16 + 16]
    tsend[4:8] = jnp.zeros((4, 128), F32)
    pl.semaphore_wait(barrier, 127)
    faces = (
        copy(tx_ref.at[pl.ds(48, 16)], trecv.at[pl.ds(0, 16)], tssem.at[0], trsem.at[0], up_x),
        copy(tsend, trecv.at[pl.ds(16, 8)], tssem.at[1], trsem.at[1], up_y),
        copy(tz_ref, trecv.at[pl.ds(24, 64)], tssem.at[2], trsem.at[2], up_z),
    )
    for face in faces:
        face.start()
    high, low = [], []
    total = jnp.zeros((64, 256), F32)
    pair = lax.broadcasted_iota(jnp.int32, (32, 256), 0)
    for j in range(16):
        weight = jnp.broadcast_to(edge[j, 0:1, :], (32, 256))
        hit = pair == jnp.broadcast_to(hir[j, 0:1, :].astype(F32).astype(jnp.int32), (32, 256))
        weight = jnp.where(hit, weight, 0.0)
        high = weight.astype(BF16)
        low = (weight - high.astype(F32)).astype(BF16)
        both = jnp.concatenate([high, low], axis=0)
        total = total + lax.dot_general(
            both, ohr[j], (((1,), (1,)), ((), ())), preferred_element_type=F32
        )
    fault = total[0:32] + total[32:64]
    acc[0:32, 0, :] = fault
    for face in faces:
        face.wait()
    shift = table_ref[0]
    for i in range(1, 16):
        shift = jnp.where(index_ref[0] == i, table_ref[i], shift)
    lane = lanes((16, 128))
    row = lax.broadcasted_iota(jnp.int32, (16, 128), 0)
    inside = [jnp.where(p > 0, 1.0, 0.0) for p in place]
    outside = [jnp.where(p < n - 1, 1.0, 0.0) for p, n in zip(place, (8, 4, 4))]
    for x in range(4):
        these = slice(x * 16, x * 16 + 16)
        upper_x = tx_ref[these] * (outside[0] if x == 3 else 1.0)
        if x == 0:
            lower_x = trecv[0:16] * inside[0]
        else:
            lower_x = tx_ref[(x - 1) * 16 : x * 16]
        ty = ty_ref[these]
        upper_y = jnp.where(row == 15, ty * outside[1], ty)
        lower_y = jnp.where(
            row == 0, trecv[16 + x : 17 + x] * inside[1], pltpu.roll(ty, 1, 0)
        )
        tz = tz_ref[these]
        upper_z = jnp.where(lane == 127, tz * outside[2], tz)
        lower_z = jnp.where(
            lane == 0,
            pltpu.roll(trecv[24 + x * 16 : 40 + x * 16], 1, 1) * inside[2],
            pltpu.roll(tz, 1, 1),
        )
        coef[0, these] = upper_x
        coef[1, these] = lower_x
        coef[2, these] = upper_y
        coef[3, these] = lower_y
        coef[4, these] = upper_z
        coef[5, these] = lower_z
        coef[6, these] = (
            upper_x + lower_x + upper_y + lower_y + upper_z + lower_z + shift * pv_ref[these]
        )
    for p in range(32):
        for parity in range(2):
            r = 2 * p + parity
            diagonal = coef[6, r : r + 1] + acc[p, 0:1, parity * 128 : parity * 128 + 128]
            coef[6, r : r + 1] = diagonal
            coef[7, r : r + 1] = 1.0 / diagonal
    both = jnp.concatenate([coef[5], coef[4]], axis=0).T
    lane = lanes((1, 128))
    edge[16, :, 0:128] = jnp.broadcast_to(
        jnp.where(lane < 64, both[0:1], both[127:128]), (8, 128)
    )
    lane = lanes((64, 128))
    coef[4] = jnp.where(lane == 127, 0.0, coef[4])
    coef[5] = jnp.where(lane == 0, 0.0, coef[5])

    def begin(r, carry):
        start = start_ref[pl.ds(r, 16, stride=64), :]
        res[r] = start
        d = start * jnp.broadcast_to(coef[7, pl.ds(r, 1)], (16, 128))
        dpad[0, 1 + r // 16, 1 + r % 16] = d
        out_ref[pl.ds(r, 16, stride=64), :] = d
        return carry

    lax.fori_loop(0, 64, begin, 0)

    def gather(j, width):
        product = jnp.dot(
            dbf[...].reshape(512, 256), ohs[j, :, 0:width], preferred_element_type=F32
        )
        tiles = []
        for h in range(width // 128):
            part = slice(h * 128, h * 128 + 128)
            hi = his[j, :, part]
            first = jnp.zeros((8, 128), F32)
            second = jnp.zeros((8, 128), F32)
            for p in range(32):
                hit = hi == p
                first = jnp.where(hit, product[p * 16 : p * 16 + 8, part], first)
                second = jnp.where(hit, product[p * 16 + 8 : p * 16 + 16, part], second)
            tiles.append((first, second))
        return tiles

    def scatter(j, tiles):
        width = 128 * len(tiles)
        for h, (first, second) in enumerate(tiles):
            part = slice(h * 128, h * 128 + 128)
            weight = edge[j, :, part]
            value = jnp.concatenate([first * weight, second * weight], axis=0).astype(BF16)
            hi = hir[j, :, part]
            for p in range(32):
                amat[p * 16 : p * 16 + 16, part] = jnp.where(
                    hi == float(p), value, jnp.zeros_like(value)
                )
        return lax.dot_general(
            amat[:, 0:width], ohr[j, :, 0:width], (((1,), (1,)), ((), ())),
            preferred_element_type=F32,
        ).reshape(32, 16, 256)

    def iterate(t, carry):
        now, gain = carry
        par = t % 2
        here = dpad.at[par]

        def halve(p, carry):
            for parity in range(2):
                r = 2 * p + parity
                dbf[p, :, parity * 128 : parity * 128 + 128] = here[
                    1 + r // 16, 1 + r % 16
                ].astype(BF16)
            return carry

        lax.fori_loop(0, 32, halve, 0)
        halos = [
            copy(here.at[4, pl.ds(1, 16)], here.at[0, pl.ds(1, 16)], hssem.at[0], hrsem.at[par, 0], up_x),
            copy(here.at[1, pl.ds(1, 16)], here.at[5, pl.ds(1, 16)], hssem.at[1], hrsem.at[par, 1], down_x),
            copy(here.at[pl.ds(1, 4), 16], here.at[pl.ds(1, 4), 0], hssem.at[2], hrsem.at[par, 2], up_y),
            copy(here.at[pl.ds(1, 4), 1], here.at[pl.ds(1, 4), 17], hssem.at[3], hrsem.at[par, 3], down_y),
        ]
        for halo in halos:
            halo.start()

        def outgoing(j, carry):
            for h, (first, second) in enumerate(gather(j, 256)):
                first, second = half_swap(first, second)
                first, second = quarter_swap(first), quarter_swap(second)
                base = j * 8 + h * 4
                send[base] = first[0:4]
                send[base + 1] = first[4:8]
                send[base + 2] = second[0:4]
                send[base + 3] = second[4:8]

            def ship(i, carry):
                slot = j * 8 + i
                copy(send.at[slot], recv.at[par, slot], ssem, rsem.at[par, j], peer(slot, place, 1)).start()
                return carry

            lax.fori_loop(0, jnp.where(j == 15, 7, 8), ship, 0)
            return carry

        lax.fori_loop(0, 16, outgoing, 0)
        recv[par, 127] = send[127]
        ((first, second),) = gather(16, 128)
        first, second = half_swap(first, second)
        zsend[0] = first
        zsend[1] = second
        halos_z = [
            copy(zsend.at[0], zrecv.at[par, 0], hssem.at[4], hrsem.at[par, 4], up_z),
            copy(zsend.at[1], zrecv.at[par, 1], hssem.at[5], hrsem.at[par, 5], down_z),
        ]
        for halo in halos_z:
            halo.start()
        for halo in halos:
            halo.wait_recv()

        def stencil(r, carry):
            x, y = 1 + r // 16, 1 + r % 16
            d = here[x, y]

            def times(which, value):
                return jnp.broadcast_to(coef[which, pl.ds(r, 1)], (16, 128)) * value

            total = times(0, here[x + 1, y]) + times(1, here[x - 1, y])
            total = total + times(2, here[x, y + 1]) + times(3, here[x, y - 1])
            total = total + times(4, pltpu.roll(d, 127, 1)) + times(5, pltpu.roll(d, 1, 1))
            res[r] = res[r] - (times(6, d) - total)
            return carry

        lax.fori_loop(0, 64, stencil, 0)
        for halo in halos_z:
            halo.wait_recv()
        tiles = half_swap(zrecv[par, 0], zrecv[par, 1])
        acc[...] = scatter(16, [tiles])

        def incoming(j, carry):
            @pl.when(j < 15)
            def _():
                copy(
                    send.at[pl.ds(0, 8)], recv.at[par, pl.ds(0, 8)], ssem, rsem.at[par, j], place
                ).wait_recv()

            @pl.when(j == 15)
            def _():
                copy(
                    send.at[pl.ds(0, 7)], recv.at[par, pl.ds(0, 7)], ssem, rsem.at[par, j], place
                ).wait_recv()

            tiles = []
            for h in range(2):
                base = j * 8 + h * 4
                first = jnp.concatenate([recv[par, base], recv[par, base + 1]], axis=0)
                second = jnp.concatenate([recv[par, base + 2], recv[par, base + 3]], axis=0)
                tiles.append(half_swap(quarter_swap(first), quarter_swap(second)))
            acc[...] += scatter(j, tiles)
            return carry

        lax.fori_loop(0, 16, incoming, 0)

        def update(p, carry):
            for parity in range(2):
                r = 2 * p + parity
                residual = res[r] + acc[p, :, parity * 128 : parity * 128 + 128]
                res[r] = residual
                inverse = jnp.broadcast_to(coef[7, pl.ds(r, 1)], (16, 128))
                x, y = 1 + r // 16, 1 + r % 16
                d = now * here[x, y] + gain * (residual * inverse)
                dpad[1 - par, x, y] = d
                out_ref[pl.ds(r, 16, stride=64), :] += d
            return carry

        lax.fori_loop(0, 32, update, 0)
        for halo in halos + halos_z:
            halo.wait_send()
        copy(send.at[pl.ds(0, 127)], recv.at[par, pl.ds(0, 127)], ssem, rsem.at[par, 0], place).wait_send()
        nxt_now, nxt_gain = carry
        for step in range(TERMS - 2):
            nxt_now = jnp.where(t == step, weights()[step + 1][0], nxt_now)
            nxt_gain = jnp.where(t == step, weights()[step + 1][1], nxt_gain)
        return nxt_now, nxt_gain

    lax.fori_loop(
        0, TERMS - 1, iterate, (jnp.float32(weights()[0][0]), jnp.float32(weights()[0][1]))
    )


def solve(start, tx, ty, tz, pv, table, index, fs, fr, ft):
    vmem = pl.BlockSpec(memory_space=pltpu.VMEM)
    smem = pl.BlockSpec(memory_space=pltpu.SMEM)
    return pl.pallas_call(
        solve_kernel,
        out_shape=jax.ShapeDtypeStruct((1024, 128), F32),
        in_specs=[vmem] * 5 + [smem] * 2 + [vmem] * 3,
        out_specs=vmem,
        scratch_shapes=[
            pltpu.VMEM((2, 6, 18, 16, 128), F32),
            pltpu.VMEM((32, 16, 256), BF16),
            pltpu.VMEM((64, 16, 128), F32),
            pltpu.VMEM((32, 16, 256), F32),
            pltpu.VMEM((512, 256), BF16),
            pltpu.VMEM((17, 256, 256), BF16),
            pltpu.VMEM((17, 256, 256), BF16),
            pltpu.VMEM((17, 8, 256), jnp.int32),
            pltpu.VMEM((17, 16, 256), BF16),
            pltpu.VMEM((1, 128, 128), F32),
            pltpu.VMEM((128, 4, 128), F32),
            pltpu.VMEM((2, 128, 4, 128), F32),
            pltpu.VMEM((2, 8, 128), F32),
            pltpu.VMEM((2, 2, 8, 128), F32),
            pltpu.VMEM((8, 64, 128), F32),
            pltpu.VMEM((17, 8, 256), F32),
            pltpu.VMEM((2, 128, 128), jnp.int32),
            pltpu.VMEM((8, 128), F32),
            pltpu.VMEM((88, 128), F32),
            pltpu.SemaphoreType.DMA,
            pltpu.SemaphoreType.DMA((2, 16)),
            pltpu.SemaphoreType.DMA((6,)),
            pltpu.SemaphoreType.DMA((2, 6)),
            pltpu.SemaphoreType.DMA((3,)),
            pltpu.SemaphoreType.DMA((3,)),
        ],
        compiler_params=pltpu.CompilerParams(
            collective_id=0, has_side_effects=True, vmem_limit_bytes=60 * 1024 * 1024
        ),
    )(start, tx, ty, tz, pv, table, index, fs, fr, ft)


def local(
    start_block, basis, trans_x, trans_y, trans_z, pore_volume, shift_table, shift_index,
    fault_send, fault_recv, fault_trans, well_cells,
):
    columns, size_x, size_y, size_z = start_block.shape
    cells = size_x * size_y * size_z
    count_x = lax.axis_size("gx")
    count_y = lax.axis_size("gy")
    count_z = lax.axis_size("gz")
    index_x = lax.axis_index("gx")
    index_y = lax.axis_index("gy")
    index_z = lax.axis_index("gz")
    full_x = size_x * count_x
    full_y = size_y * count_y
    full_z = size_z * count_z
    solution = solve(
        start_block.reshape(1024, 128),
        trans_x.reshape(64, 128),
        trans_y.reshape(64, 128),
        trans_z.reshape(64, 128),
        pore_volume.reshape(64, 128),
        shift_table,
        shift_index,
        fault_send[0],
        fault_recv[0],
        fault_trans[0],
    )
    plane = full_y * full_z
    well_x = well_cells // plane
    well_y = well_cells // full_z % full_y
    well_z = well_cells % full_z
    owned = (
        (well_x // size_x == index_x)
        & (well_y // size_y == index_y)
        & (well_z // size_z == index_z)
    )
    local_cell = (well_x % size_x * size_y + well_y % size_y) * size_z + well_z % size_z
    flat_basis = basis.reshape(basis.shape[0], cells)
    flat_x = solution.reshape(columns, cells)
    first_term = jnp.dot(
        flat_basis, flat_x.astype(jnp.bfloat16).T, preferred_element_type=jnp.float32
    )
    first_coeffs = lax.psum(first_term, ("gx", "gy", "gz"))
    first_rest = flat_x - jnp.dot(
        first_coeffs.astype(jnp.bfloat16).T, flat_basis, preferred_element_type=jnp.float32
    )
    second_term = jnp.dot(
        flat_basis, first_rest.astype(jnp.bfloat16).T, preferred_element_type=jnp.float32
    )
    second_coeffs = lax.psum(second_term, ("gx", "gy", "gz"))
    rest = first_rest - jnp.dot(
        second_coeffs.astype(jnp.bfloat16).T, flat_basis, preferred_element_type=jnp.float32
    )
    gram_term = jnp.dot(rest, rest.T, precision=lax.Precision.HIGHEST)
    gram, wells_value = lax.psum(
        (gram_term, jnp.where(owned[None, :], rest[:, local_cell], 0.0)), ("gx", "gy", "gz")
    )
    lower = jnp.linalg.cholesky(gram)
    scale = math.sqrt(full_x * full_y * full_z)
    new_flat = lax.linalg.triangular_solve(lower, rest, left_side=True, lower=True) * scale
    well_resp = (
        lax.linalg.triangular_solve(lower, wells_value, left_side=True, lower=True) * scale
    ).T
    return (
        new_flat.reshape(start_block.shape),
        first_coeffs,
        first_coeffs + second_coeffs,
        well_resp,
    )


def solution(mesh):
    in_specs = (
        P(None, "gx", "gy", "gz"),
        P(None, "gx", "gy", "gz"),
        P("gx", "gy", "gz"),
        P("gx", "gy", "gz"),
        P("gx", "gy", "gz"),
        P("gx", "gy", "gz"),
        P(),
        P(),
        P(("gx", "gy", "gz"), None, None),
        P(("gx", "gy", "gz"), None, None),
        P(("gx", "gy", "gz"), None, None),
        P(),
    )
    out_specs = (P(None, "gx", "gy", "gz"), P(), P(), P())
    return jax.shard_map(local, mesh=mesh, in_specs=in_specs, out_specs=out_specs, check_vma=False)
```

time: 1030 us -> 443 us (0.43); the launches traced: 1010 us -> 442 us
  local copies, waits for them, and re-layouts: 314 us -> 10.9 us
  other arithmetic: 251 us -> 5.88 us
  Pallas kernels: 0 us -> 213 us
  starting transfers between devices: 209 us -> 0 us
  waiting for transfers between devices: 28 us -> 0 us
    pallas_call x0 -> x1, Pallas kernels: none -> 213 us  [solve(): pl.pallas_call(solve_kernel, out_shape=jax.ShapeDtypeStruct((1024, 128),...]
    scatter-add x8 -> x0, other arithmetic: 196 us -> none  [the longest x7 174 us: local(): remote = jnp.zeros((columns, cells), jnp.float32).at[:, recv_flat].add(we...]
    ppermute x45 -> x0, starting transfers between devices: 131 us -> none  [the longest x21 77 us: extended(): before = lax.ppermute(last, axis, up)]
    gather x7 -> x0, local copies, waits for them, and re-layouts: 115 us -> none  [local(): operate_flat[:, send_flat]]
    all_to_all x7 -> x0, starting transfers between devices: 77.5 us -> none  [local(): lax.all_to_all(operate_flat[:, send_flat], ('gx', 'gy', 'gz'), split_axis...]
    all_to_all x22 -> x0, local copies, waits for them, and re-layouts: 47.2 us -> none  [local(): lax.all_to_all(operate_flat[:, send_flat], ('gx', 'gy', 'gz'), split_axis...]
    slice x32 -> x0, local copies, waits for them, and re-layouts: 28.3 us -> none  [the longest x14 16.6 us: extended(): initial = lax.slice_in_dim(value, 0, width, axis=dim)]
    ppermute x45 -> x0, waiting for transfers between devices: 28 us -> none  [the longest x21 19.4 us: extended(): after = lax.ppermute(initial, axis, down)]
  transfers between devices with their start and end apart: 52 -> 0, of which waited for: 21 -> 0; matrix products, arithmetic and copies ran while one was open for 24% -> 0% of each run, Pallas kernels for 0% -> 0%
where the time goes in v1:
time: 443 us; the launch traced here: 442 us
  Pallas kernels  213 us (48%)
  blocking collectives  192 us (43%)
  matrix products  18.3 us (4%)
  local copies, waits for them, and re-layouts  10.9 us (2%)
  other arithmetic  5.88 us (1%)
    pallas_call x1, Pallas kernels, solve(): pl.pallas_call(solve_kernel, out_shape=jax.ShapeDtypeStruct((1024, 128),...  213 us
    psum x1, blocking collectives, local(): first_coeffs = lax.psum(first_term, ('gx', 'gy', 'gz'))  66 us
    psum x1, blocking collectives, local(): lax.psum((gram_term, jnp.where(owned[None, :], rest[:, local_cell], 0.0))...  63.3 us
    psum x1, blocking collectives, local(): second_coeffs = lax.psum(second_term, ('gx', 'gy', 'gz'))  63.1 us

profile of v1, /device:TPU:1, one launch (start us, length us, event | category | flops | bytes accessed | tf_op | source)
XLA Modules:
  0.0 441.9 jit_solution(4411700376129803217)
XLA Ops:
  0.6 1.4 copy.16
  2.1 1.4 copy.17
  3.5 1.4 copy.18
  5.6 213.2 %shard_map.147 = f32[1024,128]{1,0:T(8,128)} custom-call(f32[1024,128]{1,0:T(8,128)} %bitcast.53, f32[64,128]{1,0:T(8,128)} %bitcast.58, f32[64,128]{1,0:T(8,128)} %bitcast.59, f32[64,128]{1,0:T(8,128)} %bitcast.60, f32[64,128]{1,0:T(8,128)} %bitcast.61, f32[16]{0:T(128)} %table_ref.1, s32[1]{0:T(128)S(6)} %copy.45.index_ref, s32[128,32]{1,0:T(8,128)} %bitcast.55, ...), custom_call_target="tpu_custom_call" | custom-call | tf_op jit(solution)/shard_map/pallas_call | solution.py:386
  218.8 0.0 copy-start.1
  218.8 1.1 convert_element_type.15
  219.9 0.1 convert_element_type.16
  220.0 4.5 %fusion.11 = f32[256,16]{0,1:T(8,128)S(1)} fusion(bf16[16,8192]{1,0:T(8,128)(2,1)S(1)} %convert_element_type.16, bf16[32,8,64,128]{3,2,1,0:T(8,128)(2,1)} %bitcast.49), kind=kOutput, calls=%fused_computation.15 | convolution fusion | flops 67108864 | bytes 4472832 | tf_op jit(solution)/shard_map/dot_general | solution.py:463
  224.5 66.0 %psum.28 = f32[256,16]{0,1:T(8,128)S(1)} all-reduce(f32[256,16]{0,1:T(8,128)S(1)} %fusion.11), channel_id=1, replica_groups=mesh['gx'=8,'gy'=4,'gz'=4] {'gx','gy','gz'}, use_global_device_ids=true, to_apply=%region_0.1 | all-reduce | flops 4096 | bytes 32768 | tf_op jit(solution)/shard_map/psum | solution.py:466
  290.5 0.0 copy-done.1
  290.5 0.0 copy-start.2
  290.5 0.1 reshape.50
  290.6 0.0 copy-start
  290.6 4.7 %convolution_subtract_fusion.1 = f32[16,8192]{1,0:T(8,128)S(1)} fusion(f32[16,8192]{1,0:T(8,128)S(1)} %reshape.50, bf16[32,8,64,128]{3,2,1,0:T(8,128)(2,1)} %bitcast.50, f32[256,16]{0,1:T(8,128)S(1)} %psum.28), kind=kOutput, calls=%fused_computation.3 | convolution fusion | flops 67244032 | bytes 5259264 | tf_op jit(solution)/shard_map/dot_general | solution.py:467
  295.3 0.0 copy-done
  295.3 2.3 fusion.14
  297.6 63.1 %psum.29 = f32[256,16]{0,1:T(8,128)S(1)} all-reduce(f32[256,16]{0,1:T(8,128)S(1)} %fusion.14), channel_id=1, replica_groups=mesh['gx'=8,'gy'=4,'gz'=4] {'gx','gy','gz'}, use_global_device_ids=true, to_apply=%region_1.2 | all-reduce | flops 4096 | bytes 32768 | tf_op jit(solution)/shard_map/psum | solution.py:473
  360.8 0.0 copy-start.3
  360.8 4.5 %convolution_subtract_fusion = f32[16,8192]{1,0:T(8,128)S(1)} fusion(f32[16,8192]{1,0:T(8,128)S(1)} %convolution_subtract_fusion.1, bf16[32,8,64,128]{3,2,1,0:T(8,128)(2,1)} %bitcast.51, f32[256,16]{0,1:T(8,128)S(1)} %psum.29), kind=kOutput, calls=%fused_computation.2 | convolution fusion | flops 67244032 | bytes 5259264 | tf_op jit(solution)/shard_map/dot_general | solution.py:474
  365.3 2.6 copy.21
  367.9 0.0 copy-done.3
  367.9 2.8 gather_fusion
  370.7 0.1 select_bitcast_fusion
  370.8 0.8 fusion.28
  371.6 63.3 %all-reduce = (f32[16,16]{0,1:T(8,128)S(1)}, f32[16,64]{0,1:T(8,128)S(1)}) all-reduce(f32[16,16]{0,1:T(8,128)S(1)} %fusion.28, f32[16,64]{0,1:T(8,128)S(1)} %select_bitcast_fusion), channel_id=1, replica_groups=mesh['gx'=8,'gy'=4,'gz'=4] {'gx','gy','gz'}, use_global_device_ids=true, to_apply=%region_2.3 | all-reduce | flops 1280 | bytes 10240 | tf_op jit(solution)/shard_map/psum | solution.py:478
  434.9 0.1 copy.20
  434.9 1.5 cholesky.16
  436.4 0.6 compare_reduce_fusion
  437.1 0.6 fusion.18
  437.7 1.2 custom-call.8
  439.0 0.8 convolution_multiply_fusion.1
  439.8 0.6 fusion.10
  440.4 0.9 copy.24
  441.3 0.0 copy-done.2
  441.3 0.6 add.64
  (5 shorter events, 0.1 us)
Async XLA Ops:
  218.8 71.7 %copy-start.1 = (f32[1024,128]{1,0:T(8,128)S(1)}, f32[1024,128]{1,0:T(8,128)}, u32[]{:S(2)}) copy-start(f32[1024,128]{1,0:T(8,128)} %shard_map.147) | copy-start | bytes 1572868
  290.5 150.8 %copy-start.2 = (f32[256,16]{0,1:T(8,128)}, f32[256,16]{0,1:T(8,128)S(1)}, u32[]{:S(2)}) copy-start(f32[256,16]{0,1:T(8,128)S(1)} %psum.28) | copy-start | bytes 49156
  290.6 4.7 %copy-start = (bf16[256,4,16,128]{3,2,1,0:T(8,128)(2,1)S(1)}, bf16[256,4,16,128]{3,2,1,0:T(8,128)(2,1)}, u32[]{:S(2)}) copy-start(bf16[256,4,16,128]{3,2,1,0:T(8,128)(2,1)} %param.13) | copy-start | bytes 12582916
  360.8 7.1 %copy-start.3 = (s32[64]{0:T(128)S(1)}, s32[64]{0:T(128)}, u32[]{:S(2)}) copy-start(s32[64]{0:T(128)} %param.23) | copy-start | bytes 772

commit v2 on v1

v2 whole, which is shorter than its diff:
```python
import functools
import math

import jax
import jax.numpy as jnp
from jax import lax
from jax.experimental import pallas as pl
from jax.experimental.pallas import tpu as pltpu
from jax.sharding import PartitionSpec as P

TERMS = 8
MESH = pl.DeviceIdType.MESH
F32 = jnp.float32
BF16 = jnp.bfloat16
SIGMA = 1.0 / 0.9


def weights():
    now = 1.0 / SIGMA
    table = []
    for _ in range(TERMS - 1):
        new = 1.0 / (2.0 * SIGMA - now)
        table.append((new * now, 2.0 * new / 0.9))
        now = new
    return table


def far_first():
    along = {8: (0.0, 0.5, 1.0, 1.5, 2.0, 1.5, 1.0, 0.5), 4: (0.0, 1.0, 2.0, 1.0)}
    every = [(x, y, z) for x in range(8) for y in range(4) for z in range(4)]
    return sorted(every, key=lambda o: -(along[8][o[0]] + along[4][o[1]] + along[4][o[2]]))


SLOTS = far_first()


def lanes(shape):
    return lax.broadcasted_iota(jnp.int32, shape, len(shape) - 1)


def half_swap(first, second):
    low = lanes(first.shape) < 64
    return (
        jnp.where(low, first, pltpu.roll(second, 64, 1)),
        jnp.where(low, pltpu.roll(first, 64, 1), second),
    )


def quarter_swap(value):
    upper = lax.broadcasted_iota(jnp.int32, value.shape, 0) // 4
    odd = lanes(value.shape) // 32 % 2
    moved = jnp.where(upper == 0, pltpu.roll(value, 96, 1), pltpu.roll(value, 32, 1))
    return jnp.where(upper == odd, value, pltpu.roll(moved, 4, 0))


def split(value):
    high = value.astype(BF16)
    return high, (value - high.astype(F32)).astype(BF16)


def dot_nt(a, b, **kw):
    return lax.dot_general(a, b, (((1,), (1,)), ((), ())), preferred_element_type=F32, **kw)


def solve_kernel(
    start_ref, basis_ref, tx_ref, ty_ref, tz_ref, pv_ref, table_ref, index_ref, fs_ref, fr_ref, ft_ref, wells_ref,
    out_ref, first_ref, coeffs_ref, resp_ref,
    dpad, dbf, res, xacc, acc, ohs, ohr, his, hir, wr, send, recv, zsend, zrecv, coef, edge,
    rows, tsend, trecv, bas, bt, rest, gmat, gsend, grecv, gall, gsum, csend, crecv, call, csum,
    qsend, qrecv, wsend, wrecv, wall, wsum, ohw, hiw, cmat,
    ssem, rsem, hssem, hrsem, tssem, trsem, bsem, gs1, gr1, gs2, gr2, cs1, cr1, cs2, cr2,
    qs, qr, ws1, wr1, ws2, wr2,
):
    ax, ay, az = lax.axis_index("gx"), lax.axis_index("gy"), lax.axis_index("gz")
    place = (ax, ay, az)
    me = ax * 16 + ay * 4 + az
    xs = [(ax + i) % 8 for i in range(8)]
    ys = [(ay + i) % 4 for i in range(4)]
    zs = [(az + i) % 4 for i in range(4)]

    def peer(offset):
        return (xs[offset[0] % 8], ys[offset[1] % 4], zs[offset[2] % 4])

    def opposite(offset):
        return tuple(-o for o in offset)

    def number(offset):
        x, y, z = peer(offset)
        return x * 16 + y * 4 + z

    up_x, down_x = peer((1, 0, 0)), peer((7, 0, 0))
    up_y, down_y = peer((0, 1, 0)), peer((0, 3, 0))
    up_z, down_z = peer((0, 0, 1)), peer((0, 0, 3))

    def copy(src, dst, ss, rs, where):
        return pltpu.make_async_remote_copy(
            src_ref=src, dst_ref=dst, send_sem=ss, recv_sem=rs, device_id=where, device_id_type=MESH
        )

    barrier = pltpu.get_barrier_semaphore()
    for offset in SLOTS[:127]:
        pl.semaphore_signal(barrier, inc=1, device_id=peer(offset), device_id_type=MESH)
    fetch = pltpu.make_async_copy(basis_ref, bas, bsem)
    fetch.start()

    for slot, offset in enumerate(SLOTS):
        to = number(offset)
        source = number(opposite(offset))
        rows[0, slot : slot + 1, 0:32] = fs_ref[pl.ds(to, 1), :]
        rows[1, slot : slot + 1, 0:32] = fr_ref[pl.ds(source, 1), :]
        wr[0, slot : slot + 1, 0:32] = ft_ref[pl.ds(source, 1), :]

    def flat(ref, which, half):
        lane = lanes((16, 128))
        pieces = [ref[which, pl.ds(half * 4 + q, 16, stride=8), :] for q in range(4)]
        total = pieces[0]
        for q in range(1, 4):
            total = jnp.where(lane // 32 == q, pltpu.roll(pieces[q], 32 * q, 1), total)
        return total

    column = lax.broadcasted_iota(jnp.int32, (256, 128), 0)
    for half in range(2):
        send_cells = flat(rows, 0, half)
        recv_cells = flat(rows, 1, half)
        recv_weight = flat(wr, 0, half)
        part = slice(half * 128, half * 128 + 128)
        for j in range(16):
            cell = send_cells[j : j + 1]
            his[j, :, part] = jnp.broadcast_to(cell // 256, (8, 128))
            ohs[j, :, part] = jnp.where(column == cell % 256, 1.0, 0.0).astype(BF16)
            cell = recv_cells[j : j + 1]
            place_in = slice((j % 4) * 256 + half * 128, (j % 4) * 256 + half * 128 + 128)
            hir[j // 4, :, place_in] = jnp.broadcast_to((cell // 256).astype(F32), (16, 128)).astype(BF16)
            ohr[j // 4, :, place_in] = jnp.where(column == cell % 256, 1.0, 0.0).astype(BF16)
            edge[j // 4, :, place_in] = jnp.broadcast_to(recv_weight[j : j + 1], (8, 128))
    lane = lanes((1, 128))
    line = lane % 64
    first = (line % 2) * 128
    near, far = jnp.where(lane < 64, 127, 0), jnp.where(lane < 64, 0, 127)
    his[16, :, 0:128] = jnp.broadcast_to(line // 2, (8, 128))
    hir[4, :, 0:128] = jnp.broadcast_to((line // 2).astype(F32), (16, 128)).astype(BF16)
    ohs[16, :, 0:128] = jnp.where(column == first + near, 1.0, 0.0).astype(BF16)
    ohr[4, :, 0:128] = jnp.where(column == first + far, 1.0, 0.0).astype(BF16)
    well = wells_ref[...]
    well_x, well_y, well_z = well // 32768, well // 512 % 64, well % 512
    owned = (well_x // 4 == ax) & (well_y // 16 == ay) & (well_z // 128 == az)
    cell = (well_x % 4 * 16 + well_y % 16) * 128 + well_z % 128
    hiw[...] = jnp.broadcast_to(jnp.where(owned, cell // 256, -1), (8, 128))
    ohw[...] = jnp.where(column == cell % 256, 1.0, 0.0).astype(BF16)

    def begin(i, carry):
        for u in range(4):
            p = 4 * i + u
            for parity in range(2):
                res[p, :, parity * 128 : parity * 128 + 128] = start_ref[
                    pl.ds(2 * p + parity, 16, stride=64), :
                ]
        return carry

    lax.fori_loop(0, 8, begin, 0)
    pair = lax.broadcasted_iota(jnp.int32, (32, 1024), 0)
    total = jnp.zeros((64, 256), F32)
    for j in range(4):
        weight = jnp.broadcast_to(edge[j, 0:1, :], (32, 1024))
        hit = pair == jnp.broadcast_to(hir[j, 0:1, :].astype(F32).astype(jnp.int32), (32, 1024))
        high, low = split(jnp.where(hit, weight, 0.0))
        total = total + dot_nt(jnp.concatenate([high, low], axis=0), ohr[j])
    fault = total[0:32] + total[32:64]
    acc[0:32, 0, :] = fault

    for x in range(4):
        tsend[x : x + 1] = ty_ref[x * 16 + 15 : x * 16 + 16]
    tsend[4:8] = jnp.zeros((4, 128), F32)
    pl.semaphore_wait(barrier, 127)
    faces = (
        copy(tx_ref.at[pl.ds(48, 16)], trecv.at[pl.ds(0, 16)], tssem.at[0], trsem.at[0], up_x),
        copy(tsend, trecv.at[pl.ds(16, 8)], tssem.at[1], trsem.at[1], up_y),
        copy(tz_ref, trecv.at[pl.ds(24, 64)], tssem.at[2], trsem.at[2], up_z),
    )
    for face in faces:
        face.start()
    shift = table_ref[0]
    for i in range(1, 16):
        shift = jnp.where(index_ref[0] == i, table_ref[i], shift)
    for face in faces:
        face.wait()
    lane = lanes((16, 128))
    row = lax.broadcasted_iota(jnp.int32, (16, 128), 0)
    inside = [jnp.where(p > 0, 1.0, 0.0) for p in place]
    outside = [jnp.where(p < n - 1, 1.0, 0.0) for p, n in zip(place, (8, 4, 4))]
    for x in range(4):
        these = slice(x * 16, x * 16 + 16)
        upper_x = tx_ref[these] * (outside[0] if x == 3 else 1.0)
        if x == 0:
            lower_x = trecv[0:16] * inside[0]
        else:
            lower_x = tx_ref[(x - 1) * 16 : x * 16]
        ty = ty_ref[these]
        upper_y = jnp.where(row == 15, ty * outside[1], ty)
        lower_y = jnp.where(
            row == 0, trecv[16 + x : 17 + x] * inside[1], pltpu.roll(ty, 1, 0)
        )
        tz = tz_ref[these]
        upper_z = jnp.where(lane == 127, tz * outside[2], tz)
        lower_z = jnp.where(
            lane == 0,
            pltpu.roll(trecv[24 + x * 16 : 40 + x * 16], 1, 1) * inside[2],
            pltpu.roll(tz, 1, 1),
        )
        coef[0, these] = upper_x
        coef[1, these] = lower_x
        coef[2, these] = upper_y
        coef[3, these] = lower_y
        coef[4, these] = upper_z
        coef[5, these] = lower_z
        coef[6, these] = (
            upper_x + lower_x + upper_y + lower_y + upper_z + lower_z + shift * pv_ref[these]
        )
    for p in range(32):
        for parity in range(2):
            r = 2 * p + parity
            coef[6, r : r + 1] += acc[p, 0:1, parity * 128 : parity * 128 + 128]
    coef[7] = 1.0 / coef[6]
    both = jnp.concatenate([coef[5], coef[4]], axis=0).T
    lane = lanes((1, 128))
    edge[4, :, 0:128] = jnp.broadcast_to(
        jnp.where(lane < 64, both[0:1], both[127:128]), (8, 128)
    )
    lane = lanes((64, 128))
    coef[4] = jnp.where(lane == 127, 0.0, coef[4])
    coef[5] = jnp.where(lane == 0, 0.0, coef[5])

    def initial(i, carry):
        for u in range(4):
            p = 4 * i + u
            for parity in range(2):
                part = slice(parity * 128, parity * 128 + 128)
                inverse = jnp.broadcast_to(coef[7, pl.ds(2 * p + parity, 1)], (16, 128))
                d = res[p, :, part] * inverse
                dpad[0, 1 + i // 2, 1 + (i % 2) * 8 + 2 * u + parity] = d
                dbf[p, :, part] = d.astype(BF16)
                xacc[p, :, part] = d
        return carry

    lax.fori_loop(0, 8, initial, 0)

    def pick(source, one_hot, hi_of, width):
        product = jnp.dot(source, one_hot, preferred_element_type=F32)
        tiles = []
        for h in range(width // 128):
            part = slice(h * 128, h * 128 + 128)
            hi = hi_of(part)
            first = jnp.zeros((8, 128), F32)
            second = jnp.zeros((8, 128), F32)
            for p in range(32):
                hit = hi == p
                first = jnp.where(hit, product[p * 16 : p * 16 + 8, part], first)
                second = jnp.where(hit, product[p * 16 + 8 : p * 16 + 16, part], second)
            tiles.append((first, second))
        return tiles

    def gather(j, width):
        return pick(
            dbf[...].reshape(512, 256), ohs[j, :, 0:width], lambda part: his[j, :, part], width
        )

    def scatter(j, tiles):
        width = 128 * len(tiles)
        blocks = []
        for h, (first, second) in enumerate(tiles):
            part = slice(h * 128, h * 128 + 128)
            weight = edge[j, :, part]
            value = jnp.concatenate([first * weight, second * weight], axis=0).astype(BF16)
            hi = hir[j, :, part]
            zero = jnp.zeros_like(value)
            blocks.append(
                jnp.concatenate([jnp.where(hi == float(p), value, zero) for p in range(32)], axis=0)
            )
        placed = blocks[0] if len(blocks) == 1 else jnp.concatenate(blocks, axis=1)
        return dot_nt(placed, ohr[j, :, 0:width]).reshape(32, 16, 256)

    exchange = copy(gsend.at[pl.ds(0, 127)], grecv.at[pl.ds(0, 127)], gs1, gr1, place)
    spread = copy(gsend.at[pl.ds(0, 127)], gall.at[pl.ds(0, 127)], gs2, gr2, place)

    def permute(t):
        a = lax.broadcasted_iota(jnp.int32, (256, 256), 0)
        b = lax.broadcasted_iota(jnp.int32, (256, 256), 1)
        order = jnp.where(b == a % 16 * 16 + a // 16, 1.0, 0.0).astype(BF16)

        def block(i, carry):
            k = t * 4 + i
            for q in range(2):
                sides = []
                for side in range(2):
                    base = k * 1024 + (2 * q + side) * 16
                    sides.append(
                        jnp.concatenate(
                            [bas[pl.ds(pl.multiple_of(base + 64 * kk, 16), 16), :] for kk in range(16)],
                            axis=0,
                        )
                    )
                turned = jnp.dot(
                    order, jnp.concatenate(sides, axis=1), preferred_element_type=F32
                ).astype(BF16)
                for side in range(2):
                    for xx in range(16):
                        r = (2 * q + side) * 16 + xx
                        bt[r // 2, pl.ds(pl.multiple_of(k * 16, 16), 16), r % 2 * 128 : r % 2 * 128 + 128] = (
                            turned[xx * 16 : xx * 16 + 16, side * 128 : side * 128 + 128]
                        )
            return carry

        lax.fori_loop(0, 4, block, 0)

    def iterate(t, carry):
        now, gain = carry
        par = t % 2
        here = dpad.at[par]
        halos = [
            copy(here.at[4, pl.ds(1, 16)], here.at[0, pl.ds(1, 16)], hssem.at[0], hrsem.at[par, 0], up_x),
            copy(here.at[1, pl.ds(1, 16)], here.at[5, pl.ds(1, 16)], hssem.at[1], hrsem.at[par, 1], down_x),
            copy(here.at[pl.ds(1, 4), 16], here.at[pl.ds(1, 4), 0], hssem.at[2], hrsem.at[par, 2], up_y),
            copy(here.at[pl.ds(1, 4), 1], here.at[pl.ds(1, 4), 17], hssem.at[3], hrsem.at[par, 3], down_y),
        ]
        for halo in halos:
            halo.start()
        for j in range(16):
            for h, (first, second) in enumerate(gather(j, 256)):
                first, second = half_swap(first, second)
                first, second = quarter_swap(first), quarter_swap(second)
                base = j * 8 + h * 4
                send[base] = first[0:4]
                send[base + 1] = first[4:8]
                send[base + 2] = second[0:4]
                send[base + 3] = second[4:8]
            for slot in range(j * 8, min(j * 8 + 8, 127)):
                copy(send.at[slot], recv.at[par, slot], ssem, rsem.at[par, slot // 32], peer(SLOTS[slot])).start()
        recv[par, 127] = send[127]
        ((first, second),) = gather(16, 128)
        first, second = half_swap(first, second)
        zsend[0] = first
        zsend[1] = second
        halos_z = [
            copy(zsend.at[0], zrecv.at[par, 0], hssem.at[4], hrsem.at[par, 4], up_z),
            copy(zsend.at[1], zrecv.at[par, 1], hssem.at[5], hrsem.at[par, 5], down_z),
        ]
        for halo in halos_z:
            halo.start()

        @pl.when(t == 0)
        def _():
            fetch.wait()

        @pl.when(t < 4)
        def _():
            permute(t)

        @pl.when(t == 4)
        def _():
            gmat[...] = jnp.zeros_like(gmat)

            def add(i, carry):
                total = gmat[...]
                for u in range(4):
                    total = total + dot_nt(bt[4 * i + u], bt[4 * i + u])
                gmat[...] = total
                return carry

            lax.fori_loop(0, 8, add, 0)

        @pl.when(t == 5)
        def _():
            for c in range(128):
                gsend[c] = gmat[c % 64 * 4 : c % 64 * 4 + 4, c // 64 * 128 : c // 64 * 128 + 128]
            for offset in SLOTS[:127]:
                copy(gsend.at[number(offset)], grecv.at[me], gs1, gr1, peer(offset)).start()
            grecv[me] = gsend[me]

        @pl.when(t == 6)
        def _():
            exchange.wait_recv()
            gsum[...] = jnp.sum(grecv[...], axis=0)
            for offset in SLOTS[:127]:
                copy(gsum, gall.at[me], gs2, gr2, peer(offset)).start()
            gall[me] = gsum[...]

        for halo in halos:
            halo.wait_recv()

        def stencil(i, carry):
            x = 1 + i // 4
            for u in range(4):
                r = 4 * i + u
                y = 1 + (i % 4) * 4 + u
                p, part = 2 * i + u // 2, slice(u % 2 * 128, u % 2 * 128 + 128)
                d = here[x, y]

                def times(which, value):
                    return jnp.broadcast_to(coef[which, pl.ds(r, 1)], (16, 128)) * value

                total = times(0, here[x + 1, y]) + times(1, here[x - 1, y])
                total = total + times(2, here[x, y + 1]) + times(3, here[x, y - 1])
                total = total + times(4, pltpu.roll(d, 127, 1)) + times(5, pltpu.roll(d, 1, 1))
                res[p, :, part] = res[p, :, part] - (times(6, d) - total)
            return carry

        lax.fori_loop(0, 16, stencil, 0)
        for halo in halos_z:
            halo.wait_recv()
        acc[...] = scatter(4, [half_swap(zrecv[par, 0], zrecv[par, 1])])

        def incoming(j, carry):
            @pl.when(j < 3)
            def _():
                copy(
                    send.at[pl.ds(0, 32)], recv.at[par, pl.ds(0, 32)], ssem, rsem.at[par, j], place
                ).wait_recv()

            @pl.when(j == 3)
            def _():
                copy(
                    send.at[pl.ds(0, 31)], recv.at[par, pl.ds(0, 31)], ssem, rsem.at[par, j], place
                ).wait_recv()

            tiles = []
            for h in range(8):
                base = j * 32 + h * 4
                first = jnp.concatenate([recv[par, base], recv[par, base + 1]], axis=0)
                second = jnp.concatenate([recv[par, base + 2], recv[par, base + 3]], axis=0)
                tiles.append(half_swap(quarter_swap(first), quarter_swap(second)))
            acc[...] += scatter(j, tiles)
            return carry

        lax.fori_loop(0, 4, incoming, 0)

        def update(i, carry):
            for u in range(4):
                p = 4 * i + u
                for parity in range(2):
                    part = slice(parity * 128, parity * 128 + 128)
                    residual = res[p, :, part] + acc[p, :, part]
                    res[p, :, part] = residual
                    inverse = jnp.broadcast_to(coef[7, pl.ds(2 * p + parity, 1)], (16, 128))
                    x, y = 1 + i // 2, 1 + (i % 2) * 8 + 2 * u + parity
                    d = now * here[x, y] + gain * (residual * inverse)
                    dpad[1 - par, x, y] = d
                    dbf[p, :, part] = d.astype(BF16)
                    xacc[p, :, part] += d
            return carry

        lax.fori_loop(0, 8, update, 0)
        for halo in halos + halos_z:
            halo.wait_send()
        copy(send.at[pl.ds(0, 127)], recv.at[par, pl.ds(0, 127)], ssem, rsem.at[par, 0], place).wait_send()
        nxt_now, nxt_gain = carry
        for step in range(TERMS - 2):
            nxt_now = jnp.where(t == step, weights()[step + 1][0], nxt_now)
            nxt_gain = jnp.where(t == step, weights()[step + 1][1], nxt_gain)
        return nxt_now, nxt_gain

    lax.fori_loop(
        0, TERMS - 1, iterate, (jnp.float32(weights()[0][0]), jnp.float32(weights()[0][1]))
    )

    def project(i, total):
        for u in range(4):
            p = 4 * i + u
            high, low = split(xacc[p])
            total = total + dot_nt(jnp.concatenate([high, low], axis=0), bt[p])
        return total

    total = lax.fori_loop(0, 8, project, jnp.zeros((32, 256), F32))
    for c in range(32):
        csend[c] = total[c % 16 * 2 : c % 16 * 2 + 2, c // 16 * 128 : c // 16 * 128 + 128]
    mine = ax * 4 + ay
    for offset in [o for o in SLOTS if o[2] == 0]:
        x, y = xs[offset[0]], ys[offset[1]]
        to = copy(csend.at[x * 4 + y], crecv.at[me], cs1, cr1, (x, y, y))
        if offset[:2] != (0, 0):
            to.start()
        else:

            @pl.when(az != ay)
            def _(to=to):
                to.start()

    @pl.when(az == ay)
    def _():
        crecv[me] = csend[mine]
        copy(crecv.at[pl.ds(0, 127)], crecv.at[pl.ds(0, 127)], cs1, cr1, place).wait_recv()
        csum[...] = jnp.sum(crecv[...], axis=0)
        for offset in SLOTS[:127]:
            copy(csum, call.at[mine], cs2, cr2, peer(offset)).start()
        call[mine] = csum[...]
        copy(call.at[pl.ds(0, 31)], call.at[pl.ds(0, 31)], cs2, cr2, place).wait_recv()

    @pl.when(az != ay)
    def _():
        copy(call, call, cs2, cr2, place).wait_recv()

    for c in range(32):
        cmat[c % 16 * 2 : c % 16 * 2 + 2, c // 16 * 128 : c // 16 * 128 + 128] = call[c]
    spread.wait_recv()
    for c in range(128):
        gmat[c % 64 * 4 : c % 64 * 4 + 4, c // 64 * 128 : c // 64 * 128 + 128] = gall[c]
    leading = cmat[0:16]
    first = leading.astype(BF16)
    second_sum = leading + cmat[16:32] - jnp.dot(
        first.astype(F32), gmat[...], precision=lax.Precision.HIGHEST, preferred_element_type=F32
    )
    both = jnp.concatenate([first, second_sum.astype(BF16)], axis=0)
    pad = jnp.zeros((112, 256), F32)
    first_ref[...] = jnp.concatenate([leading, pad], axis=0).T[:, 0:16]
    coeffs_ref[...] = jnp.concatenate([leading + second_sum, pad], axis=0).T[:, 0:16]

    def subtract(i, total):
        for u in range(4):
            p = 4 * i + u
            taken = jnp.dot(both, bt[p], preferred_element_type=F32)
            left = xacc[p] - taken[0:16] - taken[16:32]
            high, low = split(left)
            parts = jnp.concatenate([high, low], axis=0)
            rest[p] = parts
            total = total + dot_nt(parts, parts)
        return total

    total = lax.fori_loop(0, 8, subtract, jnp.zeros((32, 32), F32))
    gram = total[0:16, 0:16] + total[0:16, 16:32] + total[16:32, 0:16]
    lane = lanes((8, 128))
    wide = jnp.concatenate([gram, jnp.zeros((16, 112), F32)], axis=1)
    row = lax.broadcasted_iota(jnp.int32, (8, 128), 0)
    for half in range(2):
        value = wide[half * 8 : half * 8 + 8]
        line = jnp.zeros((1, 128), F32)
        for i in range(8):
            line = line + pltpu.roll(value[i : i + 1], 16 * i, 1)
        qsend[half : half + 1] = line
    for offset in SLOTS[:127]:
        copy(qsend, qrecv.at[me], qs, qr, peer(offset)).start()
    qrecv[me] = qsend[...]

    ((first_w, second_w),) = pick(
        rest[:, 0:16].reshape(512, 256), ohw[...], lambda part: hiw[...], 128
    )
    ((low_first, low_second),) = pick(
        rest[:, 16:32].reshape(512, 256), ohw[...], lambda part: hiw[...], 128
    )
    packed, _ = half_swap(first_w + low_first, second_w + low_second)
    for c in range(4):
        wsend[c] = packed[2 * c : 2 * c + 2]
    for c in range(4):

        @pl.when(~((ax == 2 * c) & (ay == c) & (az == c)))
        def _(c=c):
            copy(wsend.at[c], wrecv.at[me], ws1, wr1, (2 * c, c, c)).start()

    owner = (ax == 2 * ay) & (az == ay)

    @pl.when(owner)
    def _():
        wrecv[me] = wsend[ay]
        copy(wrecv.at[pl.ds(0, 127)], wrecv.at[pl.ds(0, 127)], ws1, wr1, place).wait_recv()
        wsum[...] = jnp.sum(wrecv[...], axis=0)
        for offset in SLOTS[:127]:
            copy(wsum, wall.at[ay], ws2, wr2, peer(offset)).start()
        wall[ay] = wsum[...]

    copy(qrecv.at[pl.ds(0, 127)], qrecv.at[pl.ds(0, 127)], qs, qr, place).wait_recv()
    sums = jnp.sum(qrecv[...], axis=0)
    pieces = []
    for half in range(2):
        for i in range(8):
            pieces.append(pltpu.roll(sums[half : half + 1], (128 - 16 * i) % 128, 1))
    gram = jnp.concatenate(pieces, axis=0)
    lane = lanes((16, 128))
    row = lax.broadcasted_iota(jnp.int32, (16, 128), 0)
    table = jnp.where(lane < 16, gram, jnp.where(lane == row + 16, 1.0, 0.0))
    for j in range(15):
        column = jnp.broadcast_to(table[:, j : j + 1], (16, 128))
        factor = jnp.where(row > j, column / column[j : j + 1], 0.0)
        table = table - factor * table[j : j + 1]
    pivot = jnp.sum(jnp.where(lane == row, table, 0.0), axis=1, keepdims=True)
    scale = 1024.0 / jnp.sqrt(pivot)
    inverse = table[:, 16:32] * scale
    high, low = split(inverse)
    factors = jnp.concatenate([high, low, high], axis=1)

    def finish(i, carry):
        for u in range(2):
            p = 2 * i + u
            parts = rest[p]
            block = jnp.dot(
                factors, jnp.concatenate([parts[0:16], parts[0:16], parts[16:32]], axis=0),
                preferred_element_type=F32,
            )
            for parity in range(2):
                out_ref[pl.ds(2 * p + parity, 16, stride=64), :] = block[
                    :, parity * 128 : parity * 128 + 128
                ]
        return carry

    lax.fori_loop(0, 16, finish, 0)

    @pl.when(owner)
    def _():
        copy(wall.at[pl.ds(0, 3)], wall.at[pl.ds(0, 3)], ws2, wr2, place).wait_recv()

    @pl.when(jnp.logical_not(owner))
    def _():
        copy(wall, wall, ws2, wr2, place).wait_recv()

    packed = jnp.concatenate([wall[c] for c in range(4)], axis=0)
    at_wells = jnp.where(lanes((16, 128)) < 64, jnp.concatenate([packed, pltpu.roll(packed, 64, 1)], axis=0), 0.0)
    answer = jnp.dot(inverse, at_wells, precision=lax.Precision.HIGHEST, preferred_element_type=F32)
    resp_ref[...] = jnp.concatenate([answer, jnp.zeros((112, 128), F32)], axis=0).T[0:64, 0:16]
    exchange.wait_send()
    copy(gall.at[pl.ds(0, 127)], gall.at[pl.ds(0, 127)], gs2, gr2, place).wait_send()
    copy(qrecv.at[pl.ds(0, 127)], qrecv.at[pl.ds(0, 127)], qs, qr, place).wait_send()

    @pl.when(az == ay)
    def _():
        copy(call.at[pl.ds(0, 31)], call.at[pl.ds(0, 31)], cs1, cr1, place).wait_send()
        copy(crecv.at[pl.ds(0, 127)], crecv.at[pl.ds(0, 127)], cs2, cr2, place).wait_send()

    @pl.when(az != ay)
    def _():
        copy(call, call, cs1, cr1, place).wait_send()

    @pl.when(owner)
    def _():
        copy(wall.at[pl.ds(0, 3)], wall.at[pl.ds(0, 3)], ws1, wr1, place).wait_send()
        copy(wrecv.at[pl.ds(0, 127)], wrecv.at[pl.ds(0, 127)], ws2, wr2, place).wait_send()

    @pl.when(jnp.logical_not(owner))
    def _():
        copy(wall, wall, ws1, wr1, place).wait_send()


def solve(*args):
    vmem = pl.BlockSpec(memory_space=pltpu.VMEM)
    smem = pl.BlockSpec(memory_space=pltpu.SMEM)
    dma = pltpu.SemaphoreType.DMA
    return pl.pallas_call(
        solve_kernel,
        out_shape=(
            jax.ShapeDtypeStruct((1024, 128), F32),
            jax.ShapeDtypeStruct((256, 16), F32),
            jax.ShapeDtypeStruct((256, 16), F32),
            jax.ShapeDtypeStruct((64, 16), F32),
        ),
        in_specs=[vmem, pl.BlockSpec(memory_space=pl.ANY)] + [vmem] * 4 + [smem] * 2 + [vmem] * 4,
        out_specs=(vmem,) * 4,
        scratch_shapes=[
            pltpu.VMEM((2, 6, 18, 16, 128), F32),
            pltpu.VMEM((32, 16, 256), BF16),
            pltpu.VMEM((32, 16, 256), F32),
            pltpu.VMEM((32, 16, 256), F32),
            pltpu.VMEM((32, 16, 256), F32),
            pltpu.VMEM((17, 256, 256), BF16),
            pltpu.VMEM((5, 256, 1024), BF16),
            pltpu.VMEM((17, 8, 256), jnp.int32),
            pltpu.VMEM((5, 16, 1024), BF16),
            pltpu.VMEM((1, 128, 128), F32),
            pltpu.VMEM((128, 4, 128), F32),
            pltpu.VMEM((2, 128, 4, 128), F32),
            pltpu.VMEM((2, 8, 128), F32),
            pltpu.VMEM((2, 2, 8, 128), F32),
            pltpu.VMEM((8, 64, 128), F32),
            pltpu.VMEM((5, 8, 1024), F32),
            pltpu.VMEM((2, 128, 128), jnp.int32),
            pltpu.VMEM((8, 128), F32),
            pltpu.VMEM((88, 128), F32),
            pltpu.VMEM((16384, 128), BF16),
            pltpu.VMEM((32, 256, 256), BF16),
            pltpu.VMEM((32, 32, 256), BF16),
            pltpu.VMEM((256, 256), F32),
            pltpu.VMEM((128, 4, 128), F32),
            pltpu.VMEM((128, 4, 128), F32),
            pltpu.VMEM((128, 4, 128), F32),
            pltpu.VMEM((4, 128), F32),
            pltpu.VMEM((32, 2, 128), F32),
            pltpu.VMEM((128, 2, 128), F32),
            pltpu.VMEM((32, 2, 128), F32),
            pltpu.VMEM((2, 128), F32),
            pltpu.VMEM((2, 128), F32),
            pltpu.VMEM((128, 2, 128), F32),
            pltpu.VMEM((4, 2, 128), F32),
            pltpu.VMEM((128, 2, 128), F32),
            pltpu.VMEM((4, 2, 128), F32),
            pltpu.VMEM((2, 128), F32),
            pltpu.VMEM((256, 128), BF16),
            pltpu.VMEM((8, 128), jnp.int32),
            pltpu.VMEM((32, 256), F32),
            dma,
            dma((2, 4)),
            dma((6,)),
            dma((2, 6)),
            dma((3,)),
            dma((3,)),
        ]
        + [dma] * 15,
        compiler_params=pltpu.CompilerParams(
            collective_id=0, has_side_effects=True, vmem_limit_bytes=60 * 1024 * 1024
        ),
    )(*args)


def local(
    start_block, basis, trans_x, trans_y, trans_z, pore_volume, shift_table, shift_index,
    fault_send, fault_recv, fault_trans, well_cells,
):
    wells = jnp.concatenate([well_cells, well_cells]).reshape(1, 128)
    new_block, first_coeffs, coeffs, well_resp = solve(
        start_block.reshape(1024, 128),
        basis.reshape(16384, 128),
        trans_x.reshape(64, 128),
        trans_y.reshape(64, 128),
        trans_z.reshape(64, 128),
        pore_volume.reshape(64, 128),
        shift_table,
        shift_index,
        fault_send[0],
        fault_recv[0],
        fault_trans[0],
        wells,
    )
    return new_block.reshape(start_block.shape), first_coeffs, coeffs, well_resp


def solution(mesh):
    in_specs = (
        P(None, "gx", "gy", "gz"),
        P(None, "gx", "gy", "gz"),
        P("gx", "gy", "gz"),
        P("gx", "gy", "gz"),
        P("gx", "gy", "gz"),
        P("gx", "gy", "gz"),
        P(),
        P(),
        P(("gx", "gy", "gz"), None, None),
        P(("gx", "gy", "gz"), None, None),
        P(("gx", "gy", "gz"), None, None),
        P(),
    )
    out_specs = (P(None, "gx", "gy", "gz"), P(), P(), P())
    return jax.shard_map(local, mesh=mesh, in_specs=in_specs, out_specs=out_specs, check_vma=False)
```

time: 443 us -> 158 us (0.36)
  blocking collectives: 192 us -> 0 us
  Pallas kernels: 213 us -> 144 us
  matrix products: 18.3 us -> 0 us
  other arithmetic: 5.88 us -> 1.32 us
    psum x3 -> x0, blocking collectives: 192 us -> none  [the longest x1 66 us: local(): first_coeffs = lax.psum(first_term, ('gx', 'gy', 'gz'))]
    pallas_call x1, Pallas kernels: 213 us -> 144 us  [solve(): pl.pallas_call(solve_kernel, out_shape=(jax.ShapeDtypeStruct((1024, 128),...]
    dot_general x5 -> x0, matrix products: 16.8 us -> none  [the longest x1 4.67 us: local(): jnp.dot(first_coeffs.astype(jnp.bfloat16).T, flat_basis, preferred_elemen...]
    unnamed x12 -> x7, local copies, waits for them, and re-layouts: 5.23 us -> 10.8 us
where the time goes in v2:
time: 158 us
  Pallas kernels  144 us (91%)
  local copies, waits for them, and re-layouts  10.8 us (7%)
    pallas_call x1, Pallas kernels, solve(): pl.pallas_call(solve_kernel, out_shape=(jax.ShapeDtypeStruct((1024, 128),...  144 us
    unnamed x7, local copies, waits for them, and re-layouts  10.8 us

profile of v2, /device:TPU:1, one launch (start us, length us, event | category | flops | bytes accessed | tf_op | source)
XLA Modules:
  0.0 157.9 jit_solution(11450015361390354814)
XLA Ops:
  1.3 1.3 add_bitcast_fusion.wells_ref
  2.6 1.4 copy.16
  4.0 1.4 copy.17
  5.5 1.4 copy.18
  6.9 144.5 %shard_map.147 = (f32[1024,128]{1,0:T(8,128)}, f32[256,16]{1,0:T(8,128)}, f32[256,16]{1,0:T(8,128)}, f32[64,16]{1,0:T(8,128)}) custom-call(f32[1024,128]{1,0:T(8,128)} %bitcast.13, bf16[16384,128]{1,0:T(8,128)(2,1)} %bitcast.12, f32[64,128]{1,0:T(8,128)} %bitcast.18, f32[64,128]{1,0:T(8,128)} %bitcast.19, f32[64,128]{1,0:T(8,128)} %bitcast.20, ...), custom_call_target="tpu_custom_call" | custom-call | tf_op jit(solution)/shard_map/pallas_call | solution.py:643
  151.4 1.4 copy.21
  152.8 1.6 %copy.19 = f32[256,16]{0,1:T(8,128)} copy(f32[256,16]{1,0:T(8,128)} %get-tuple-element.13) | data formatting | bytes 32768
  154.4 1.6 %copy.20 = f32[256,16]{0,1:T(8,128)} copy(f32[256,16]{1,0:T(8,128)} %get-tuple-element.14) | data formatting | bytes 32768
  156.0 1.9 %copy.24 = f32[16,4,16,128]{3,2,1,0:T(8,128)} copy(f32[16,4,16,128]{3,2,1,0:T(8,128)} %bitcast.14) | data formatting | bytes 1048576

commit v3 on v2

--- a/solution.py
+++ b/solution.py
@@ -3,6 +3,7 @@
 
 import jax
 import jax.numpy as jnp
+import numpy as np
 from jax import lax
 from jax.experimental import pallas as pl
 from jax.experimental.pallas import tpu as pltpu
@@ -63,10 +64,10 @@
 
 
 def solve_kernel(
-    start_ref, basis_ref, tx_ref, ty_ref, tz_ref, pv_ref, table_ref, index_ref, fs_ref, fr_ref, ft_ref, wells_ref,
-    out_ref, first_ref, coeffs_ref, resp_ref,
-    dpad, dbf, res, xacc, acc, ohs, ohr, his, hir, wr, send, recv, zsend, zrecv, coef, edge,
-    rows, tsend, trecv, bas, bt, rest, gmat, gsend, grecv, gall, gsum, csend, crecv, call, csum,
+    start_ref, basis_ref, tx_ref, ty_ref, tz_ref, pv_ref, table_ref, index_ref, fs_ref, fr_ref, ft_ref, wells_ref, offs_ref,
+    rest, factors_ref, first_ref, coeffs_ref, resp_ref,
+    dpad, dbf, res, xacc, acc, ohs, ohr, his, hir, mk, mkz, send, recv, zsend, zrecv, coef, edge,
+    rows, tsend, trecv, bas, bt, gmat, gsend, grecv, gall, gsum, csend, crecv, call, csum,
     qsend, qrecv, wsend, wrecv, wall, wsum, ohw, hiw, cmat,
     ssem, rsem, hssem, hrsem, tssem, trsem, bsem, gs1, gr1, gs2, gr2, cs1, cr1, cs2, cr2,
     qs, qr, ws1, wr1, ws2, wr2,
@@ -81,9 +82,6 @@
     def peer(offset):
         return (xs[offset[0] % 8], ys[offset[1] % 4], zs[offset[2] % 4])
 
-    def opposite(offset):
-        return tuple(-o for o in offset)
-
     def number(offset):
         x, y, z = peer(offset)
         return x * 16 + y * 4 + z
@@ -103,50 +101,81 @@
     fetch = pltpu.make_async_copy(basis_ref, bas, bsem)
     fetch.start()
 
-    for slot, offset in enumerate(SLOTS):
-        to = number(offset)
-        source = number(opposite(offset))
-        rows[0, slot : slot + 1, 0:32] = fs_ref[pl.ds(to, 1), :]
-        rows[1, slot : slot + 1, 0:32] = fr_ref[pl.ds(source, 1), :]
-        wr[0, slot : slot + 1, 0:32] = ft_ref[pl.ds(source, 1), :]
-
-    def flat(ref, which, half):
+    offs = offs_ref[...]
+    spot = lax.broadcasted_iota(jnp.int32, (128, 128), 0)
+
+    def order_of(sign):
+        x, y, z = (offs[i : i + 1] * sign for i in range(3))
+        target = (x + ax + 8) % 8 * 16 + (y + ay + 4) % 4 * 4 + (z + az + 4) % 4
+        return jnp.where(spot == target, 1.0, 0.0).astype(BF16)
+
+    def spread_rows(which, value):
+        rows[which] = jnp.concatenate([value] * 4, axis=0).T
+
+    def halves(ref, order, which):
+        cells = ref[...]
+        parts = jnp.concatenate([cells // 256, cells % 256], axis=0).astype(F32).astype(BF16)
+        moved = jnp.dot(parts, order, preferred_element_type=F32)
+        spread_rows(which, moved[0:32])
+        spread_rows(which + 1, moved[32:64])
+
+    halves(fs_ref, order_of(1), 0)
+    source_order = order_of(-1)
+    halves(fr_ref, source_order, 2)
+    high, low = split(ft_ref[...])
+    lowest = (ft_ref[...] - high.astype(F32) - low.astype(F32)).astype(BF16)
+    moved = jnp.dot(
+        jnp.concatenate([high, low, lowest], axis=0), source_order, preferred_element_type=F32
+    )
+    spread_rows(4, moved[0:32] + moved[32:64] + moved[64:96])
+
+    def flat(which, half):
         lane = lanes((16, 128))
-        pieces = [ref[which, pl.ds(half * 4 + q, 16, stride=8), :] for q in range(4)]
+        pieces = [rows[which, pl.ds(half * 4 + q, 16, stride=8), :] for q in range(4)]
         total = pieces[0]
         for q in range(1, 4):
-            total = jnp.where(lane // 32 == q, pltpu.roll(pieces[q], 32 * q, 1), total)
+            total = jnp.where(lane // 32 == q, pieces[q], total)
         return total
 
-    column = lax.broadcasted_iota(jnp.int32, (256, 128), 0)
+    def mask(hi, p):
+        one = jnp.where(hi == float(p), 1.0, 0.0)
+        return jnp.concatenate([one, one], axis=0).astype(BF16)
+
+    column = lax.broadcasted_iota(jnp.int32, (256, 128), 0).astype(F32)
+
+    def one_hot(low):
+        return jnp.where(column == low, 1.0, 0.0).astype(BF16)
+
     for half in range(2):
-        send_cells = flat(rows, 0, half)
-        recv_cells = flat(rows, 1, half)
-        recv_weight = flat(wr, 0, half)
+        send_hi, send_lo, recv_hi, recv_lo, recv_weight = (flat(i, half) for i in range(5))
         part = slice(half * 128, half * 128 + 128)
         for j in range(16):
-            cell = send_cells[j : j + 1]
-            his[j, :, part] = jnp.broadcast_to(cell // 256, (8, 128))
-            ohs[j, :, part] = jnp.where(column == cell % 256, 1.0, 0.0).astype(BF16)
-            cell = recv_cells[j : j + 1]
+            this = slice(j, j + 1)
+            his[j, :, part] = jnp.broadcast_to(send_hi[this], (8, 128))
+            ohs[j, :, part] = one_hot(send_lo[this])
             place_in = slice((j % 4) * 256 + half * 128, (j % 4) * 256 + half * 128 + 128)
-            hir[j // 4, :, place_in] = jnp.broadcast_to((cell // 256).astype(F32), (16, 128)).astype(BF16)
-            ohr[j // 4, :, place_in] = jnp.where(column == cell % 256, 1.0, 0.0).astype(BF16)
-            edge[j // 4, :, place_in] = jnp.broadcast_to(recv_weight[j : j + 1], (8, 128))
+            hi = jnp.broadcast_to(recv_hi[this], (8, 128))
+            hir[j // 4, :, place_in] = hi
+            for p in range(32):
+                mk[j // 4, p, :, place_in] = mask(hi, p)
+            ohr[j // 4, :, place_in] = one_hot(recv_lo[this])
+            edge[j // 4, :, place_in] = jnp.broadcast_to(recv_weight[this], (8, 128))
     lane = lanes((1, 128))
     line = lane % 64
     first = (line % 2) * 128
     near, far = jnp.where(lane < 64, 127, 0), jnp.where(lane < 64, 0, 127)
-    his[16, :, 0:128] = jnp.broadcast_to(line // 2, (8, 128))
-    hir[4, :, 0:128] = jnp.broadcast_to((line // 2).astype(F32), (16, 128)).astype(BF16)
-    ohs[16, :, 0:128] = jnp.where(column == first + near, 1.0, 0.0).astype(BF16)
-    ohr[4, :, 0:128] = jnp.where(column == first + far, 1.0, 0.0).astype(BF16)
+    hi = jnp.broadcast_to((line // 2).astype(F32), (8, 128))
+    his[16, :, 0:128] = hi
+    for p in range(32):
+        mkz[p] = mask(hi, p)
+    ohs[16, :, 0:128] = one_hot((first + near).astype(F32))
+    ohr[4, :, 0:128] = one_hot((first + far).astype(F32))
     well = wells_ref[...]
     well_x, well_y, well_z = well // 32768, well // 512 % 64, well % 512
     owned = (well_x // 4 == ax) & (well_y // 16 == ay) & (well_z // 128 == az)
     cell = (well_x % 4 * 16 + well_y % 16) * 128 + well_z % 128
-    hiw[...] = jnp.broadcast_to(jnp.where(owned, cell // 256, -1), (8, 128))
-    ohw[...] = jnp.where(column == cell % 256, 1.0, 0.0).astype(BF16)
+    hiw[...] = jnp.broadcast_to(jnp.where(owned, cell // 256, -1).astype(F32), (8, 128))
+    ohw[...] = one_hot((cell % 256).astype(F32))
 
     def begin(i, carry):
         for u in range(4):
@@ -158,11 +187,11 @@
         return carry
 
     lax.fori_loop(0, 8, begin, 0)
-    pair = lax.broadcasted_iota(jnp.int32, (32, 1024), 0)
+    pair = lax.broadcasted_iota(jnp.int32, (32, 1024), 0).astype(F32)
     total = jnp.zeros((64, 256), F32)
     for j in range(4):
         weight = jnp.broadcast_to(edge[j, 0:1, :], (32, 1024))
-        hit = pair == jnp.broadcast_to(hir[j, 0:1, :].astype(F32).astype(jnp.int32), (32, 1024))
+        hit = pair == jnp.broadcast_to(hir[j, 0:1, :], (32, 1024))
         high, low = split(jnp.where(hit, weight, 0.0))
         total = total + dot_nt(jnp.concatenate([high, low], axis=0), ohr[j])
     fault = total[0:32] + total[32:64]
@@ -253,7 +282,7 @@
             first = jnp.zeros((8, 128), F32)
             second = jnp.zeros((8, 128), F32)
             for p in range(32):
-                hit = hi == p
+                hit = hi == float(p)
                 first = jnp.where(hit, product[p * 16 : p * 16 + 8, part], first)
                 second = jnp.where(hit, product[p * 16 + 8 : p * 16 + 16, part], second)
             tiles.append((first, second))
@@ -265,19 +294,14 @@
         )
 
     def scatter(j, tiles):
-        width = 128 * len(tiles)
-        blocks = []
+        values = []
         for h, (first, second) in enumerate(tiles):
-            part = slice(h * 128, h * 128 + 128)
-            weight = edge[j, :, part]
-            value = jnp.concatenate([first * weight, second * weight], axis=0).astype(BF16)
-            hi = hir[j, :, part]
-            zero = jnp.zeros_like(value)
-            blocks.append(
-                jnp.concatenate([jnp.where(hi == float(p), value, zero) for p in range(32)], axis=0)
-            )
-        placed = blocks[0] if len(blocks) == 1 else jnp.concatenate(blocks, axis=1)
-        return dot_nt(placed, ohr[j, :, 0:width]).reshape(32, 16, 256)
+            weight = edge[j, :, h * 128 : h * 128 + 128]
+            values.append(jnp.concatenate([first * weight, second * weight], axis=0).astype(BF16))
+        value = values[0] if len(values) == 1 else jnp.concatenate(values, axis=1)
+        masks = mkz if j == 4 else mk.at[j]
+        placed = jnp.concatenate([masks[p] * value for p in range(32)], axis=0)
+        return dot_nt(placed, ohr[j, :, 0 : 128 * len(tiles)]).reshape(32, 16, 256)
 
     exchange = copy(gsend.at[pl.ds(0, 127)], grecv.at[pl.ds(0, 127)], gs1, gr1, place)
     spread = copy(gsend.at[pl.ds(0, 127)], gall.at[pl.ds(0, 127)], gs2, gr2, place)
@@ -324,29 +348,49 @@
         ]
         for halo in halos:
             halo.start()
-        for j in range(16):
-            for h, (first, second) in enumerate(gather(j, 256)):
-                first, second = half_swap(first, second)
-                first, second = quarter_swap(first), quarter_swap(second)
-                base = j * 8 + h * 4
-                send[base] = first[0:4]
-                send[base + 1] = first[4:8]
-                send[base + 2] = second[0:4]
-                send[base + 3] = second[4:8]
-            for slot in range(j * 8, min(j * 8 + 8, 127)):
-                copy(send.at[slot], recv.at[par, slot], ssem, rsem.at[par, slot // 32], peer(SLOTS[slot])).start()
-        recv[par, 127] = send[127]
-        ((first, second),) = gather(16, 128)
-        first, second = half_swap(first, second)
-        zsend[0] = first
-        zsend[1] = second
+
+        def stencil(r):
+            x, y = 1 + r // 16, 1 + r % 16
+            p, part = r // 2, slice(r % 2 * 128, r % 2 * 128 + 128)
+            d = here[x, y]
+
+            def times(which, value):
+                return jnp.broadcast_to(coef[which, r : r + 1], (16, 128)) * value
+
+            total = times(4, pltpu.roll(d, 127, 1)) + times(5, pltpu.roll(d, 1, 1))
+            for which, inside_too, near in (
+                (0, x < 4, (x + 1, y)), (1, x > 1, (x - 1, y)), (2, y < 16, (x, y + 1)), (3, y > 1, (x, y - 1))
+            ):
+                if inside_too:
+                    total = total + times(which, here[near])
+            res[p, :, part] = res[p, :, part] - (times(6, d) - total)
+
         halos_z = [
             copy(zsend.at[0], zrecv.at[par, 0], hssem.at[4], hrsem.at[par, 4], up_z),
             copy(zsend.at[1], zrecv.at[par, 1], hssem.at[5], hrsem.at[par, 5], down_z),
         ]
-        for halo in halos_z:
-            halo.start()
-
+        for chunk in range(4):
+            for j in range(chunk * 4, chunk * 4 + 4):
+                for h, (first, second) in enumerate(gather(j, 256)):
+                    first, second = half_swap(first, second)
+                    first, second = quarter_swap(first), quarter_swap(second)
+                    base = j * 8 + h * 4
+                    send[base] = first[0:4]
+                    send[base + 1] = first[4:8]
+                    send[base + 2] = second[0:4]
+                    send[base + 3] = second[4:8]
+            if chunk == 2:
+                ((first, second),) = gather(16, 128)
+                first, second = half_swap(first, second)
+                zsend[0] = first
+                zsend[1] = second
+                for halo in halos_z:
+                    halo.start()
+            for slot in range(chunk * 32, min(chunk * 32 + 32, 127)):
+                copy(send.at[slot], recv.at[par, slot], ssem, rsem.at[par, chunk], peer(SLOTS[slot])).start()
+        recv[par, 127] = send[127]
+        for r in range(64):
+            stencil(r)
         @pl.when(t == 0)
         def _():
             fetch.wait()
@@ -387,51 +431,33 @@
         for halo in halos:
             halo.wait_recv()
 
-        def stencil(i, carry):
-            x = 1 + i // 4
-            for u in range(4):
-                r = 4 * i + u
-                y = 1 + (i % 4) * 4 + u
-                p, part = 2 * i + u // 2, slice(u % 2 * 128, u % 2 * 128 + 128)
-                d = here[x, y]
-
-                def times(which, value):
-                    return jnp.broadcast_to(coef[which, pl.ds(r, 1)], (16, 128)) * value
-
-                total = times(0, here[x + 1, y]) + times(1, here[x - 1, y])
-                total = total + times(2, here[x, y + 1]) + times(3, here[x, y - 1])
-                total = total + times(4, pltpu.roll(d, 127, 1)) + times(5, pltpu.roll(d, 1, 1))
-                res[p, :, part] = res[p, :, part] - (times(6, d) - total)
-            return carry
-
-        lax.fori_loop(0, 16, stencil, 0)
+        for y in range(16):
+            for x, which, beyond in ((0, 1, 0), (3, 0, 5)):
+                r = x * 16 + y
+                p, part = r // 2, slice(r % 2 * 128, r % 2 * 128 + 128)
+                res[p, :, part] += jnp.broadcast_to(coef[which, r : r + 1], (16, 128)) * here[beyond, 1 + y]
+        for x in range(4):
+            for y, which, beyond in ((0, 3, 0), (15, 2, 17)):
+                r = x * 16 + y
+                p, part = r // 2, slice(r % 2 * 128, r % 2 * 128 + 128)
+                res[p, :, part] += jnp.broadcast_to(coef[which, r : r + 1], (16, 128)) * here[1 + x, beyond]
         for halo in halos_z:
             halo.wait_recv()
-        acc[...] = scatter(4, [half_swap(zrecv[par, 0], zrecv[par, 1])])
-
-        def incoming(j, carry):
-            @pl.when(j < 3)
-            def _():
-                copy(
-                    send.at[pl.ds(0, 32)], recv.at[par, pl.ds(0, 32)], ssem, rsem.at[par, j], place
-                ).wait_recv()
-
-            @pl.when(j == 3)
-            def _():
-                copy(
-                    send.at[pl.ds(0, 31)], recv.at[par, pl.ds(0, 31)], ssem, rsem.at[par, j], place
-                ).wait_recv()
-
+        for j in range(4):
+            count = 32 if j < 3 else 31
+            copy(
+                send.at[pl.ds(0, count)], recv.at[par, pl.ds(0, count)], ssem, rsem.at[par, j], place
+            ).wait_recv()
             tiles = []
             for h in range(8):
                 base = j * 32 + h * 4
                 first = jnp.concatenate([recv[par, base], recv[par, base + 1]], axis=0)
                 second = jnp.concatenate([recv[par, base + 2], recv[par, base + 3]], axis=0)
                 tiles.append(half_swap(quarter_swap(first), quarter_swap(second)))
-            acc[...] += scatter(j, tiles)
-            return carry
-
-        lax.fori_loop(0, 4, incoming, 0)
+            if j == 0:
+                acc[...] = scatter(4, [half_swap(zrecv[par, 0], zrecv[par, 1])]) + scatter(j, tiles)
+            else:
+                acc[...] += scatter(j, tiles)
 
         def update(i, carry):
             for u in range(4):
@@ -484,6 +510,10 @@
             def _(to=to):
                 to.start()
 
+    spread.wait_recv()
+    for c in range(128):
+        gmat[c % 64 * 4 : c % 64 * 4 + 4, c // 64 * 128 : c // 64 * 128 + 128] = gall[c]
+
     @pl.when(az == ay)
     def _():
         crecv[me] = csend[mine]
@@ -500,18 +530,14 @@
 
     for c in range(32):
         cmat[c % 16 * 2 : c % 16 * 2 + 2, c // 16 * 128 : c // 16 * 128 + 128] = call[c]
-    spread.wait_recv()
-    for c in range(128):
-        gmat[c % 64 * 4 : c % 64 * 4 + 4, c // 64 * 128 : c // 64 * 128 + 128] = gall[c]
     leading = cmat[0:16]
     first = leading.astype(BF16)
     second_sum = leading + cmat[16:32] - jnp.dot(
         first.astype(F32), gmat[...], precision=lax.Precision.HIGHEST, preferred_element_type=F32
     )
     both = jnp.concatenate([first, second_sum.astype(BF16)], axis=0)
-    pad = jnp.zeros((112, 256), F32)
-    first_ref[...] = jnp.concatenate([leading, pad], axis=0).T[:, 0:16]
-    coeffs_ref[...] = jnp.concatenate([leading + second_sum, pad], axis=0).T[:, 0:16]
+    first_ref[...] = leading
+    coeffs_ref[...] = leading + second_sum
 
     def subtract(i, total):
         for u in range(4):
@@ -583,23 +609,7 @@
     scale = 1024.0 / jnp.sqrt(pivot)
     inverse = table[:, 16:32] * scale
     high, low = split(inverse)
-    factors = jnp.concatenate([high, low, high], axis=1)
-
-    def finish(i, carry):
-        for u in range(2):
-            p = 2 * i + u
-            parts = rest[p]
-            block = jnp.dot(
-                factors, jnp.concatenate([parts[0:16], parts[0:16], parts[16:32]], axis=0),
-                preferred_element_type=F32,
-            )
-            for parity in range(2):
-                out_ref[pl.ds(2 * p + parity, 16, stride=64), :] = block[
-                    :, parity * 128 : parity * 128 + 128
-                ]
-        return carry
-
-    lax.fori_loop(0, 16, finish, 0)
+    factors_ref[...] = jnp.concatenate([high, low, high], axis=1)
 
     @pl.when(owner)
     def _():
@@ -612,7 +622,7 @@
     packed = jnp.concatenate([wall[c] for c in range(4)], axis=0)
     at_wells = jnp.where(lanes((16, 128)) < 64, jnp.concatenate([packed, pltpu.roll(packed, 64, 1)], axis=0), 0.0)
     answer = jnp.dot(inverse, at_wells, precision=lax.Precision.HIGHEST, preferred_element_type=F32)
-    resp_ref[...] = jnp.concatenate([answer, jnp.zeros((112, 128), F32)], axis=0).T[0:64, 0:16]
+    resp_ref[...] = answer[:, 0:64]
     exchange.wait_send()
     copy(gall.at[pl.ds(0, 127)], gall.at[pl.ds(0, 127)], gs2, gr2, place).wait_send()
     copy(qrecv.at[pl.ds(0, 127)], qrecv.at[pl.ds(0, 127)], qs, qr, place).wait_send()
@@ -643,13 +653,14 @@
     return pl.pallas_call(
         solve_kernel,
         out_shape=(
-            jax.ShapeDtypeStruct((1024, 128), F32),
-            jax.ShapeDtypeStruct((256, 16), F32),
-            jax.ShapeDtypeStruct((256, 16), F32),
-            jax.ShapeDtypeStruct((64, 16), F32),
+            jax.ShapeDtypeStruct((32, 32, 256), BF16),
+            jax.ShapeDtypeStruct((16, 48), BF16),
+            jax.ShapeDtypeStruct((16, 256), F32),
+            jax.ShapeDtypeStruct((16, 256), F32),
+            jax.ShapeDtypeStruct((16, 64), F32),
         ),
-        in_specs=[vmem, pl.BlockSpec(memory_space=pl.ANY)] + [vmem] * 4 + [smem] * 2 + [vmem] * 4,
-        out_specs=(vmem,) * 4,
+        in_specs=[vmem, pl.BlockSpec(memory_space=pl.ANY)] + [vmem] * 4 + [smem] * 2 + [vmem] * 5,
+        out_specs=(vmem,) * 5,
         scratch_shapes=[
             pltpu.VMEM((2, 6, 18, 16, 128), F32),
             pltpu.VMEM((32, 16, 256), BF16),
@@ -658,21 +669,21 @@
             pltpu.VMEM((32, 16, 256), F32),
             pltpu.VMEM((17, 256, 256), BF16),
             pltpu.VMEM((5, 256, 1024), BF16),
-            pltpu.VMEM((17, 8, 256), jnp.int32),
-            pltpu.VMEM((5, 16, 1024), BF16),
-            pltpu.VMEM((1, 128, 128), F32),
+            pltpu.VMEM((17, 8, 256), F32),
+            pltpu.VMEM((4, 8, 1024), F32),
+            pltpu.VMEM((4, 32, 16, 1024), BF16),
+            pltpu.VMEM((32, 16, 128), BF16),
             pltpu.VMEM((128, 4, 128), F32),
             pltpu.VMEM((2, 128, 4, 128), F32),
             pltpu.VMEM((2, 8, 128), F32),
             pltpu.VMEM((2, 2, 8, 128), F32),
             pltpu.VMEM((8, 64, 128), F32),
             pltpu.VMEM((5, 8, 1024), F32),
-            pltpu.VMEM((2, 128, 128), jnp.int32),
+            pltpu.VMEM((5, 128, 128), F32),
             pltpu.VMEM((8, 128), F32),
             pltpu.VMEM((88, 128), F32),
             pltpu.VMEM((16384, 128), BF16),
             pltpu.VMEM((32, 256, 256), BF16),
-            pltpu.VMEM((32, 32, 256), BF16),
             pltpu.VMEM((256, 256), F32),
             pltpu.VMEM((128, 4, 128), F32),
             pltpu.VMEM((128, 4, 128), F32),
@@ -689,7 +700,7 @@
             pltpu.VMEM((4, 2, 128), F32),
             pltpu.VMEM((2, 128), F32),
             pltpu.VMEM((256, 128), BF16),
-            pltpu.VMEM((8, 128), jnp.int32),
+            pltpu.VMEM((8, 128), F32),
             pltpu.VMEM((32, 256), F32),
             dma,
             dma((2, 4)),
@@ -705,12 +716,54 @@
     )(*args)
 
 
+def finish_kernel(
+    rest_ref, factors_ref, first_in, coeffs_in, resp_in, out_ref, first_ref, coeffs_ref, resp_ref
+):
+    first_ref[...] = first_in[...]
+    coeffs_ref[...] = coeffs_in[...]
+    resp_ref[...] = resp_in[...]
+    factors = factors_ref[...]
+
+    def finish(i, carry):
+        for u in range(4):
+            p = 4 * i + u
+            parts = rest_ref[p]
+            block = jnp.dot(
+                factors, jnp.concatenate([parts[0:16], parts[0:16], parts[16:32]], axis=0),
+                preferred_element_type=F32,
+            )
+            for parity in range(2):
+                out_ref[pl.ds(2 * p + parity, 16, stride=64), :] = block[
+                    :, parity * 128 : parity * 128 + 128
+                ]
+        return carry
+
+    lax.fori_loop(0, 8, finish, 0)
+
+
+def finish(*args):
+    vmem = pl.BlockSpec(memory_space=pltpu.VMEM)
+    return pl.pallas_call(
+        finish_kernel,
+        out_shape=(
+            jax.ShapeDtypeStruct((1024, 128), F32),
+            jax.ShapeDtypeStruct((16, 256), F32),
+            jax.ShapeDtypeStruct((16, 256), F32),
+            jax.ShapeDtypeStruct((16, 64), F32),
+        ),
+        in_specs=[vmem] * 5,
+        out_specs=(vmem,) * 4,
+    )(*args)
+
+
 def local(
     start_block, basis, trans_x, trans_y, trans_z, pore_volume, shift_table, shift_index,
     fault_send, fault_recv, fault_trans, well_cells,
 ):
     wells = jnp.concatenate([well_cells, well_cells]).reshape(1, 128)
-    new_block, first_coeffs, coeffs, well_resp = solve(
+    offsets = np.zeros((8, 128), np.int32)
+    offsets[0:3] = np.array(SLOTS, np.int32).T
+    parts = solve(
         start_block.reshape(1024, 128),
         basis.reshape(16384, 128),
         trans_x.reshape(64, 128),
@@ -719,12 +772,14 @@
         pore_volume.reshape(64, 128),
         shift_table,
         shift_index,
-        fault_send[0],
-        fault_recv[0],
-        fault_trans[0],
+        fault_send[0].T,
+        fault_recv[0].T,
+        fault_trans[0].T,
         wells,
-    )
-    return new_block.reshape(start_block.shape), first_coeffs, coeffs, well_resp
+        jnp.asarray(offsets),
+    )
+    new_block, first_coeffs, coeffs, well_resp = finish(*parts)
+    return new_block.reshape(start_block.shape), first_coeffs.T, coeffs.T, well_resp.T
 
 
 def solution(mesh):

time: 158 us -> 139 us (0.88)
  local copies, waits for them, and re-layouts: 10.8 us -> 0 us
  Pallas kernels: 144 us -> 136 us
    unnamed x7 -> x0, local copies, waits for them, and re-layouts: 10.8 us -> none
    pallas_call x1 -> x2, Pallas kernels: 144 us -> 136 us  [the longest x1 133 us: solve(): pl.pallas_call(solve_kernel, out_shape=(jax.ShapeDtypeStruct((32, 32, 256...]
where the time goes in v3:
time: 139 us
  Pallas kernels  136 us (98%)
    pallas_call x1, Pallas kernels, solve(): pl.pallas_call(solve_kernel, out_shape=(jax.ShapeDtypeStruct((32, 32, 256...  133 us
    pallas_call x1, Pallas kernels, finish(): pl.pallas_call(finish_kernel, out_shape=(jax.ShapeDtypeStruct((1024, 128)...  3.13 us

profile of v3, /device:TPU:1, one launch (start us, length us, event | category | flops | bytes accessed | tf_op | source)
XLA Modules:
  0.0 139.1 jit_solution(14381618910190334973)
XLA Ops:
  1.3 1.3 add_bitcast_fusion.wells_ref
  2.6 133.3 %shard_map.156 = (bf16[32,32,256]{2,1,0:T(8,128)(2,1)}, bf16[16,48]{1,0:T(8,128)(2,1)}, f32[16,256]{1,0:T(8,128)}, f32[16,256]{1,0:T(8,128)}, f32[16,64]{1,0:T(8,128)}) custom-call(f32[1024,128]{1,0:T(8,128)} %bitcast.22, bf16[16384,128]{1,0:T(8,128)(2,1)} %bitcast.21, f32[64,128]{1,0:T(8,128)} %bitcast.23, f32[64,128]{1,0:T(8,128)} %bitcast.24, ...), custom_call_target="tpu_custom_call" | custom-call | tf_op jit(solution)/shard_map/pallas_call | solution.py:653
  135.9 3.1 %shard_map.157 = (f32[1024,128]{1,0:T(8,128)}, f32[16,256]{1,0:T(8,128)}, f32[16,256]{1,0:T(8,128)}, f32[16,64]{1,0:T(8,128)}) custom-call(bf16[32,32,256]{2,1,0:T(8,128)(2,1)} %get-tuple-element.13.rest_ref, bf16[16,48]{1,0:T(8,128)(2,1)} %get-tuple-element.14.factors_ref, f32[16,256]{1,0:T(8,128)} %get-tuple-element.15.first_in, ...), custom_call_target="tpu_custom_call" | custom-call | tf_op jit(solution)/shard_map/pallas_call | solution.py:746

commit v4 on v3

--- a/solution.py
+++ b/solution.py
@@ -66,8 +66,8 @@
 def solve_kernel(
     start_ref, basis_ref, tx_ref, ty_ref, tz_ref, pv_ref, table_ref, index_ref, fs_ref, fr_ref, ft_ref, wells_ref, offs_ref,
     rest, factors_ref, first_ref, coeffs_ref, resp_ref,
-    dpad, dbf, res, xacc, acc, ohs, ohr, his, hir, mk, mkz, send, recv, zsend, zrecv, coef, edge,
-    rows, tsend, trecv, bas, bt, gmat, gsend, grecv, gall, gsum, csend, crecv, call, csum,
+    dpad, dbf, res, xacc, acc, ohs, ohr, his, hir, mk, send, recv, zsend, zrecv, coef, edge,
+    rows, tsend, trecv, bas, bt, gmat, gfull, gsend, grecv, gall, gsum, csend, crecv, call, csum,
     qsend, qrecv, wsend, wrecv, wall, wsum, ohw, hiw, cmat,
     ssem, rsem, hssem, hrsem, tssem, trsem, bsem, gs1, gr1, gs2, gr2, cs1, cr1, cs2, cr2,
     qs, qr, ws1, wr1, ws2, wr2,
@@ -151,25 +151,30 @@
         part = slice(half * 128, half * 128 + 128)
         for j in range(16):
             this = slice(j, j + 1)
-            his[j, :, part] = jnp.broadcast_to(send_hi[this], (8, 128))
-            ohs[j, :, part] = one_hot(send_lo[this])
+            quad = jnp.floor(send_hi[this] * 0.5)
+            his[j, :, part] = jnp.broadcast_to(quad, (8, 128))
+            low = send_lo[this] + (send_hi[this] - 2.0 * quad) * 256.0
+            ohs[j, half, 0:256] = one_hot(low)
+            ohs[j, half, 256:512] = one_hot(low - 256.0)
             place_in = slice((j % 4) * 256 + half * 128, (j % 4) * 256 + half * 128 + 128)
             hi = jnp.broadcast_to(recv_hi[this], (8, 128))
             hir[j // 4, :, place_in] = hi
             for p in range(32):
-                mk[j // 4, p, :, place_in] = mask(hi, p)
-            ohr[j // 4, :, place_in] = one_hot(recv_lo[this])
+                mk[2 * j + half, p] = mask(hi, p)
+            ohr[2 * j + half] = one_hot(recv_lo[this])
             edge[j // 4, :, place_in] = jnp.broadcast_to(recv_weight[this], (8, 128))
     lane = lanes((1, 128))
     line = lane % 64
     first = (line % 2) * 128
     near, far = jnp.where(lane < 64, 127, 0), jnp.where(lane < 64, 0, 127)
     hi = jnp.broadcast_to((line // 2).astype(F32), (8, 128))
-    his[16, :, 0:128] = hi
     for p in range(32):
-        mkz[p] = mask(hi, p)
-    ohs[16, :, 0:128] = one_hot((first + near).astype(F32))
-    ohr[4, :, 0:128] = one_hot((first + far).astype(F32))
+        mk[32, p] = mask(hi, p)
+    ohr[32] = one_hot((first + far).astype(F32))
+    his[16, :, 0:128] = jnp.broadcast_to((line // 4).astype(F32), (8, 128))
+    low = ((line % 4) * 128 + near).astype(F32)
+    ohs[16, 0, 0:256] = one_hot(low)
+    ohs[16, 0, 256:512] = one_hot(low - 256.0)
     well = wells_ref[...]
     well_x, well_y, well_z = well // 32768, well // 512 % 64, well % 512
     owned = (well_x // 4 == ax) & (well_y // 16 == ay) & (well_z // 128 == az)
@@ -193,7 +198,10 @@
         weight = jnp.broadcast_to(edge[j, 0:1, :], (32, 1024))
         hit = pair == jnp.broadcast_to(hir[j, 0:1, :], (32, 1024))
         high, low = split(jnp.where(hit, weight, 0.0))
-        total = total + dot_nt(jnp.concatenate([high, low], axis=0), ohr[j])
+        total = total + dot_nt(
+            jnp.concatenate([high, low], axis=0),
+            jnp.concatenate([ohr[8 * j + h] for h in range(8)], axis=1),
+        )
     fault = total[0:32] + total[32:64]
     acc[0:32, 0, :] = fault
 
@@ -267,13 +275,13 @@
                 inverse = jnp.broadcast_to(coef[7, pl.ds(2 * p + parity, 1)], (16, 128))
                 d = res[p, :, part] * inverse
                 dpad[0, 1 + i // 2, 1 + (i % 2) * 8 + 2 * u + parity] = d
-                dbf[p, :, part] = d.astype(BF16)
-                xacc[p, :, part] = d
+                dbf[u % 2 * 2 + parity, pl.ds(pl.multiple_of((2 * i + u // 2) * 16, 16), 16)] = d.astype(BF16)
+                xacc[p, :, part] = jnp.zeros_like(d)
         return carry
 
     lax.fori_loop(0, 8, initial, 0)
 
-    def pick(source, one_hot, hi_of, width):
+    def pick(source, one_hot, hi_of, width, count):
         product = jnp.dot(source, one_hot, preferred_element_type=F32)
         tiles = []
         for h in range(width // 128):
@@ -281,7 +289,7 @@
             hi = hi_of(part)
             first = jnp.zeros((8, 128), F32)
             second = jnp.zeros((8, 128), F32)
-            for p in range(32):
+            for p in range(count):
                 hit = hi == float(p)
                 first = jnp.where(hit, product[p * 16 : p * 16 + 8, part], first)
                 second = jnp.where(hit, product[p * 16 + 8 : p * 16 + 16, part], second)
@@ -289,8 +297,11 @@
         return tiles
 
     def gather(j, width):
+        picks = [ohs[j, h] for h in range(width // 128)]
         return pick(
-            dbf[...].reshape(512, 256), ohs[j, :, 0:width], lambda part: his[j, :, part], width
+            jnp.concatenate([dbf[q] for q in range(4)], axis=1),
+            picks[0] if len(picks) == 1 else jnp.concatenate(picks, axis=1),
+            lambda part: his[j, :, part], width, 16,
         )
 
     def scatter(j, tiles):
@@ -298,10 +309,17 @@
         for h, (first, second) in enumerate(tiles):
             weight = edge[j, :, h * 128 : h * 128 + 128]
             values.append(jnp.concatenate([first * weight, second * weight], axis=0).astype(BF16))
-        value = values[0] if len(values) == 1 else jnp.concatenate(values, axis=1)
-        masks = mkz if j == 4 else mk.at[j]
-        placed = jnp.concatenate([masks[p] * value for p in range(32)], axis=0)
-        return dot_nt(placed, ohr[j, :, 0 : 128 * len(tiles)]).reshape(32, 16, 256)
+        picks = [ohr[8 * j + h] for h in range(len(values))]
+        picks = picks[0] if len(picks) == 1 else jnp.concatenate(picks, axis=1)
+        sums = []
+        for side in range(2):
+            placed = [
+                jnp.concatenate([mk[8 * j + h, side * 16 + p] * value for p in range(16)], axis=0)
+                for h, value in enumerate(values)
+            ]
+            placed = placed[0] if len(placed) == 1 else jnp.concatenate(placed, axis=1)
+            sums.append(dot_nt(placed, picks).reshape(16, 16, 256))
+        return sums
 
     exchange = copy(gsend.at[pl.ds(0, 127)], grecv.at[pl.ds(0, 127)], gs1, gr1, place)
     spread = copy(gsend.at[pl.ds(0, 127)], gall.at[pl.ds(0, 127)], gs2, gr2, place)
@@ -312,7 +330,7 @@
         order = jnp.where(b == a % 16 * 16 + a // 16, 1.0, 0.0).astype(BF16)
 
         def block(i, carry):
-            k = t * 4 + i
+            k = t * 6 + i
             for q in range(2):
                 sides = []
                 for side in range(2):
@@ -334,7 +352,7 @@
                         )
             return carry
 
-        lax.fori_loop(0, 4, block, 0)
+        lax.fori_loop(0, jnp.where(t < 2, 6, 4), block, 0)
 
     def iterate(t, carry):
         now, gain = carry
@@ -353,6 +371,7 @@
             x, y = 1 + r // 16, 1 + r % 16
             p, part = r // 2, slice(r % 2 * 128, r % 2 * 128 + 128)
             d = here[x, y]
+            xacc[p, :, part] += d
 
             def times(which, value):
                 return jnp.broadcast_to(coef[which, r : r + 1], (16, 128)) * value
@@ -369,8 +388,8 @@
             copy(zsend.at[0], zrecv.at[par, 0], hssem.at[4], hrsem.at[par, 4], up_z),
             copy(zsend.at[1], zrecv.at[par, 1], hssem.at[5], hrsem.at[par, 5], down_z),
         ]
-        for chunk in range(4):
-            for j in range(chunk * 4, chunk * 4 + 4):
+        for group in (range(0, 2), range(2, 8), range(8, 16)):
+            for j in group:
                 for h, (first, second) in enumerate(gather(j, 256)):
                     first, second = half_swap(first, second)
                     first, second = quarter_swap(first), quarter_swap(second)
@@ -379,15 +398,17 @@
                     send[base + 1] = first[4:8]
                     send[base + 2] = second[0:4]
                     send[base + 3] = second[4:8]
-            if chunk == 2:
+            if group[0] == 8:
                 ((first, second),) = gather(16, 128)
                 first, second = half_swap(first, second)
                 zsend[0] = first
                 zsend[1] = second
                 for halo in halos_z:
                     halo.start()
-            for slot in range(chunk * 32, min(chunk * 32 + 32, 127)):
-                copy(send.at[slot], recv.at[par, slot], ssem, rsem.at[par, chunk], peer(SLOTS[slot])).start()
+            for slot in range(group[0] * 8, min(group[-1] * 8 + 8, 127)):
+                copy(
+                    send.at[slot], recv.at[par, slot], ssem, rsem.at[par, slot // 32], peer(SLOTS[slot])
+                ).start()
         recv[par, 127] = send[127]
         for r in range(64):
             stencil(r)
@@ -395,27 +416,49 @@
         def _():
             fetch.wait()
 
-        @pl.when(t < 4)
+        @pl.when(t < 3)
         def _():
             permute(t)
 
+        @pl.when(t == 3)
+        def _():
+            gfull[...] = jnp.zeros_like(gfull)
+
+            def add(i, carry):
+                total = gfull[...]
+                for u in range(4):
+                    total = total + dot_nt(bt[4 * i + u], bt[4 * i + u])
+                gfull[...] = total
+                return carry
+
+            lax.fori_loop(0, 8, add, 0)
+            gmat[0] = gfull[0:128, 0:128]
+            gmat[1] = gfull[0:128, 128:256]
+            gmat[2] = gfull[128:256, 128:256]
+
         @pl.when(t == 4)
         def _():
-            gmat[...] = jnp.zeros_like(gmat)
-
-            def add(i, carry):
-                total = gmat[...]
+            gfull[:, 0:128] = jnp.zeros((256, 128), F32)
+
+            def at_wells(i, carry):
+                total = gfull[:, 0:128]
                 for u in range(4):
-                    total = total + dot_nt(bt[4 * i + u], bt[4 * i + u])
-                gmat[...] = total
+                    p = 4 * i + u
+                    hit = hiw[0:1] == lax.convert_element_type(p, F32)
+                    found = jnp.dot(bt[p], ohw[...], preferred_element_type=F32)
+                    total = total + jnp.where(hit, found, 0.0)
+                gfull[:, 0:128] = total
                 return carry
 
-            lax.fori_loop(0, 8, add, 0)
+            lax.fori_loop(0, 8, at_wells, 0)
+            gmat[3] = jnp.where(
+                lanes((128, 128)) < 64, gfull[0:128, 0:128], gfull[128:256, 0:128]
+            )
 
         @pl.when(t == 5)
         def _():
             for c in range(128):
-                gsend[c] = gmat[c % 64 * 4 : c % 64 * 4 + 4, c // 64 * 128 : c // 64 * 128 + 128]
+                gsend[c] = gmat[c // 32, c % 32 * 4 : c % 32 * 4 + 4]
             for offset in SLOTS[:127]:
                 copy(gsend.at[number(offset)], grecv.at[me], gs1, gr1, peer(offset)).start()
             grecv[me] = gsend[me]
@@ -443,7 +486,9 @@
                 res[p, :, part] += jnp.broadcast_to(coef[which, r : r + 1], (16, 128)) * here[1 + x, beyond]
         for halo in halos_z:
             halo.wait_recv()
-        for j in range(4):
+        for side, value in enumerate(scatter(4, [half_swap(zrecv[par, 0], zrecv[par, 1])])):
+            acc[side * 16 : side * 16 + 16] = value
+        for j in (3, 2, 1, 0):
             count = 32 if j < 3 else 31
             copy(
                 send.at[pl.ds(0, count)], recv.at[par, pl.ds(0, count)], ssem, rsem.at[par, j], place
@@ -454,27 +499,19 @@
                 first = jnp.concatenate([recv[par, base], recv[par, base + 1]], axis=0)
                 second = jnp.concatenate([recv[par, base + 2], recv[par, base + 3]], axis=0)
                 tiles.append(half_swap(quarter_swap(first), quarter_swap(second)))
-            if j == 0:
-                acc[...] = scatter(4, [half_swap(zrecv[par, 0], zrecv[par, 1])]) + scatter(j, tiles)
-            else:
-                acc[...] += scatter(j, tiles)
-
-        def update(i, carry):
-            for u in range(4):
-                p = 4 * i + u
-                for parity in range(2):
-                    part = slice(parity * 128, parity * 128 + 128)
-                    residual = res[p, :, part] + acc[p, :, part]
-                    res[p, :, part] = residual
-                    inverse = jnp.broadcast_to(coef[7, pl.ds(2 * p + parity, 1)], (16, 128))
-                    x, y = 1 + i // 2, 1 + (i % 2) * 8 + 2 * u + parity
-                    d = now * here[x, y] + gain * (residual * inverse)
-                    dpad[1 - par, x, y] = d
-                    dbf[p, :, part] = d.astype(BF16)
-                    xacc[p, :, part] += d
-            return carry
-
-        lax.fori_loop(0, 8, update, 0)
+            sums = scatter(j, tiles)
+            if j:
+                for side, value in enumerate(sums):
+                    acc[side * 16 : side * 16 + 16] += value
+        for r in range(64):
+            p, part = r // 2, slice(r % 2 * 128, r % 2 * 128 + 128)
+            residual = res[p, :, part] + acc[p, :, part] + sums[p // 16][p % 16, :, part]
+            res[p, :, part] = residual
+            inverse = jnp.broadcast_to(coef[7, r : r + 1], (16, 128))
+            x, y = 1 + r // 16, 1 + r % 16
+            d = now * here[x, y] + gain * (residual * inverse)
+            dpad[1 - par, x, y] = d
+            dbf[r % 4, r // 4 * 16 : r // 4 * 16 + 16] = d.astype(BF16)
         for halo in halos + halos_z:
             halo.wait_send()
         copy(send.at[pl.ds(0, 127)], recv.at[par, pl.ds(0, 127)], ssem, rsem.at[par, 0], place).wait_send()
@@ -489,13 +526,18 @@
     )
 
     def project(i, total):
-        for u in range(4):
-            p = 4 * i + u
-            high, low = split(xacc[p])
-            total = total + dot_nt(jnp.concatenate([high, low], axis=0), bt[p])
+        for u in range(8):
+            p = 8 * i + u
+            d = jnp.concatenate([dpad[1, 1 + i, 1 + 2 * u], dpad[1, 1 + i, 2 + 2 * u]], axis=1)
+            x = xacc[p] + d
+            xacc[p] = x
+            high, low = split(x)
+            parts = jnp.concatenate([high, low], axis=0)
+            rest[p] = parts
+            total = total + dot_nt(parts, bt[p])
         return total
 
-    total = lax.fori_loop(0, 8, project, jnp.zeros((32, 256), F32))
+    total = lax.fori_loop(0, 4, project, jnp.zeros((32, 256), F32))
     for c in range(32):
         csend[c] = total[c % 16 * 2 : c % 16 * 2 + 2, c // 16 * 128 : c // 16 * 128 + 128]
     mine = ax * 4 + ay
@@ -510,9 +552,35 @@
             def _(to=to):
                 to.start()
 
+    ((first_w, second_w),) = pick(
+        rest[:, 0:16].reshape(512, 256), ohw[...], lambda part: hiw[...], 128, 32
+    )
+    ((low_first, low_second),) = pick(
+        rest[:, 16:32].reshape(512, 256), ohw[...], lambda part: hiw[...], 128, 32
+    )
+    packed, _ = half_swap(first_w + low_first, second_w + low_second)
+    for c in range(4):
+        wsend[c] = packed[2 * c : 2 * c + 2]
+    for c in range(4):
+
+        @pl.when(~((ax == 2 * c) & (ay == c) & (az == (c + 1) % 4)))
+        def _(c=c):
+            copy(wsend.at[c], wrecv.at[me], ws1, wr1, (2 * c, c, (c + 1) % 4)).start()
+
+    owner = (ax == 2 * ay) & (az == (ay + 1) % 4)
+
+    @pl.when(owner)
+    def _():
+        wrecv[me] = wsend[ay]
+        copy(wrecv.at[pl.ds(0, 127)], wrecv.at[pl.ds(0, 127)], ws1, wr1, place).wait_recv()
+        wsum[...] = jnp.sum(wrecv[...], axis=0)
+        for offset in SLOTS[:127]:
+            copy(wsum, wall.at[ay], ws2, wr2, peer(offset)).start()
+        wall[ay] = wsum[...]
+
     spread.wait_recv()
     for c in range(128):
-        gmat[c % 64 * 4 : c % 64 * 4 + 4, c // 64 * 128 : c // 64 * 128 + 128] = gall[c]
+        gmat[c // 32, c % 32 * 4 : c % 32 * 4 + 4] = gall[c]
 
     @pl.when(az == ay)
     def _():
@@ -532,16 +600,25 @@
         cmat[c % 16 * 2 : c % 16 * 2 + 2, c // 16 * 128 : c // 16 * 128 + 128] = call[c]
     leading = cmat[0:16]
     first = leading.astype(BF16)
-    second_sum = leading + cmat[16:32] - jnp.dot(
-        first.astype(F32), gmat[...], precision=lax.Precision.HIGHEST, preferred_element_type=F32
-    )
+    exact = dict(precision=lax.Precision.HIGHEST)
+    wide = first.astype(F32)
+    near, far = wide[:, 0:128], wide[:, 128:256]
+    taken = jnp.concatenate(
+        [
+            jnp.dot(near, gmat[0], preferred_element_type=F32, **exact) + dot_nt(far, gmat[1], **exact),
+            jnp.dot(near, gmat[1], preferred_element_type=F32, **exact)
+            + jnp.dot(far, gmat[2], preferred_element_type=F32, **exact),
+        ],
+        axis=1,
+    )
+    second_sum = leading + cmat[16:32] - taken
     both = jnp.concatenate([first, second_sum.astype(BF16)], axis=0)
     first_ref[...] = leading
     coeffs_ref[...] = leading + second_sum
 
     def subtract(i, total):
-        for u in range(4):
-            p = 4 * i + u
+        for u in range(8):
+            p = 8 * i + u
             taken = jnp.dot(both, bt[p], preferred_element_type=F32)
             left = xacc[p] - taken[0:16] - taken[16:32]
             high, low = split(left)
@@ -550,7 +627,7 @@
             total = total + dot_nt(parts, parts)
         return total
 
-    total = lax.fori_loop(0, 8, subtract, jnp.zeros((32, 32), F32))
+    total = lax.fori_loop(0, 4, subtract, jnp.zeros((32, 32), F32))
     gram = total[0:16, 0:16] + total[0:16, 16:32] + total[16:32, 0:16]
     lane = lanes((8, 128))
     wide = jnp.concatenate([gram, jnp.zeros((16, 112), F32)], axis=1)
@@ -564,32 +641,6 @@
     for offset in SLOTS[:127]:
         copy(qsend, qrecv.at[me], qs, qr, peer(offset)).start()
     qrecv[me] = qsend[...]
-
-    ((first_w, second_w),) = pick(
-        rest[:, 0:16].reshape(512, 256), ohw[...], lambda part: hiw[...], 128
-    )
-    ((low_first, low_second),) = pick(
-        rest[:, 16:32].reshape(512, 256), ohw[...], lambda part: hiw[...], 128
-    )
-    packed, _ = half_swap(first_w + low_first, second_w + low_second)
-    for c in range(4):
-        wsend[c] = packed[2 * c : 2 * c + 2]
-    for c in range(4):
-
-        @pl.when(~((ax == 2 * c) & (ay == c) & (az == c)))
-        def _(c=c):
-            copy(wsend.at[c], wrecv.at[me], ws1, wr1, (2 * c, c, c)).start()
-
-    owner = (ax == 2 * ay) & (az == ay)
-
-    @pl.when(owner)
-    def _():
-        wrecv[me] = wsend[ay]
-        copy(wrecv.at[pl.ds(0, 127)], wrecv.at[pl.ds(0, 127)], ws1, wr1, place).wait_recv()
-        wsum[...] = jnp.sum(wrecv[...], axis=0)
-        for offset in SLOTS[:127]:
-            copy(wsum, wall.at[ay], ws2, wr2, peer(offset)).start()
-        wall[ay] = wsum[...]
 
     copy(qrecv.at[pl.ds(0, 127)], qrecv.at[pl.ds(0, 127)], qs, qr, place).wait_recv()
     sums = jnp.sum(qrecv[...], axis=0)
@@ -621,6 +672,11 @@
 
     packed = jnp.concatenate([wall[c] for c in range(4)], axis=0)
     at_wells = jnp.where(lanes((16, 128)) < 64, jnp.concatenate([packed, pltpu.roll(packed, 64, 1)], axis=0), 0.0)
+    at_basis = gmat[3].astype(BF16)
+    taken = jnp.dot(both[:, 0:128], at_basis, preferred_element_type=F32) + pltpu.roll(
+        jnp.dot(both[:, 128:256], at_basis, preferred_element_type=F32), 64, 1
+    )
+    at_wells = jnp.where(lanes((16, 128)) < 64, at_wells - taken[0:16] - taken[16:32], 0.0)
     answer = jnp.dot(inverse, at_wells, precision=lax.Precision.HIGHEST, preferred_element_type=F32)
     resp_ref[...] = answer[:, 0:64]
     exchange.wait_send()
@@ -663,16 +719,15 @@
         out_specs=(vmem,) * 5,
         scratch_shapes=[
             pltpu.VMEM((2, 6, 18, 16, 128), F32),
-            pltpu.VMEM((32, 16, 256), BF16),
+            pltpu.VMEM((4, 256, 128), BF16),
             pltpu.VMEM((32, 16, 256), F32),
             pltpu.VMEM((32, 16, 256), F32),
             pltpu.VMEM((32, 16, 256), F32),
-            pltpu.VMEM((17, 256, 256), BF16),
-            pltpu.VMEM((5, 256, 1024), BF16),
+            pltpu.VMEM((17, 2, 512, 128), BF16),
+            pltpu.VMEM((33, 256, 128), BF16),
             pltpu.VMEM((17, 8, 256), F32),
             pltpu.VMEM((4, 8, 1024), F32),
-            pltpu.VMEM((4, 32, 16, 1024), BF16),
-            pltpu.VMEM((32, 16, 128), BF16),
+            pltpu.VMEM((33, 32, 16, 128), BF16),
             pltpu.VMEM((128, 4, 128), F32),
             pltpu.VMEM((2, 128, 4, 128), F32),
             pltpu.VMEM((2, 8, 128), F32),
@@ -684,6 +739,7 @@
             pltpu.VMEM((88, 128), F32),
             pltpu.VMEM((16384, 128), BF16),
             pltpu.VMEM((32, 256, 256), BF16),
+            pltpu.VMEM((4, 128, 128), F32),
             pltpu.VMEM((256, 256), F32),
             pltpu.VMEM((128, 4, 128), F32),
             pltpu.VMEM((128, 4, 128), F32),

time: 139 us -> 124 us (0.89)
  Pallas kernels: 136 us -> 122 us
    pallas_call x1, Pallas kernels: 133 us -> 118 us  [solve(): pl.pallas_call(solve_kernel, out_shape=(jax.ShapeDtypeStruct((32, 32, 256...]
where the time goes in v4:
time: 124 us
  Pallas kernels  122 us (98%)
  other arithmetic  1.31 us (1%)
  between operations  1.29 us (1%)
    pallas_call x1, Pallas kernels, solve(): pl.pallas_call(solve_kernel, out_shape=(jax.ShapeDtypeStruct((32, 32, 256...  118 us
    pallas_call x1, Pallas kernels, finish(): pl.pallas_call(finish_kernel, out_shape=(jax.ShapeDtypeStruct((1024, 128)...  3.13 us

profile of v4, /device:TPU:1, one launch (start us, length us, event | category | flops | bytes accessed | tf_op | source)
XLA Modules:
  0.0 124.2 jit_solution(10628914237845236185)
XLA Ops:
  1.3 1.3 %add_bitcast_fusion.wells_ref = s32[1,128]{1,0:T(1,128)} fusion(s32[64]{0:T(128)} %param.24), kind=kLoop, calls=%fused_computation | loop fusion | flops 128 | bytes 768 | tf_op jit(solution)/shard_map/reshape | solution.py:819
  2.6 118.5 %shard_map.156 = (bf16[32,32,256]{2,1,0:T(8,128)(2,1)}, bf16[16,48]{1,0:T(8,128)(2,1)}, f32[16,256]{1,0:T(8,128)}, f32[16,256]{1,0:T(8,128)}, f32[16,64]{1,0:T(8,128)}) custom-call(f32[1024,128]{1,0:T(8,128)} %bitcast.22, bf16[16384,128]{1,0:T(8,128)(2,1)} %bitcast.21, f32[64,128]{1,0:T(8,128)} %bitcast.23, f32[64,128]{1,0:T(8,128)} %bitcast.24, ...), custom_call_target="tpu_custom_call" | custom-call | tf_op jit(solution)/shard_map/pallas_call | solution.py:709
  121.1 3.1 %shard_map.157 = (f32[1024,128]{1,0:T(8,128)}, f32[16,256]{1,0:T(8,128)}, f32[16,256]{1,0:T(8,128)}, f32[16,64]{1,0:T(8,128)}) custom-call(bf16[32,32,256]{2,1,0:T(8,128)(2,1)} %get-tuple-element.13.rest_ref, bf16[16,48]{1,0:T(8,128)(2,1)} %get-tuple-element.14.factors_ref, f32[16,256]{1,0:T(8,128)} %get-tuple-element.15.first_in, ...), custom_call_target="tpu_custom_call" | custom-call | tf_op jit(solution)/shard_map/pallas_call | solution.py:802

commit v5 on v4

--- a/solution.py
+++ b/solution.py
@@ -66,7 +66,7 @@
 def solve_kernel(
     start_ref, basis_ref, tx_ref, ty_ref, tz_ref, pv_ref, table_ref, index_ref, fs_ref, fr_ref, ft_ref, wells_ref, offs_ref,
     rest, factors_ref, first_ref, coeffs_ref, resp_ref,
-    dpad, dbf, res, xacc, acc, ohs, ohr, his, hir, mk, send, recv, zsend, zrecv, coef, edge,
+    dpad, dbf, res, xacc, acc, ohs, ohr, his, hir, hiz, mk, send, recv, zsend, zrecv, coef, edge,
     rows, tsend, trecv, bas, bt, gmat, gfull, gsend, grecv, gall, gsum, csend, crecv, call, csum,
     qsend, qrecv, wsend, wrecv, wall, wsum, ohw, hiw, cmat,
     ssem, rsem, hssem, hrsem, tssem, trsem, bsem, gs1, gr1, gs2, gr2, cs1, cr1, cs2, cr2,
@@ -159,8 +159,6 @@
             place_in = slice((j % 4) * 256 + half * 128, (j % 4) * 256 + half * 128 + 128)
             hi = jnp.broadcast_to(recv_hi[this], (8, 128))
             hir[j // 4, :, place_in] = hi
-            for p in range(32):
-                mk[2 * j + half, p] = mask(hi, p)
             ohr[2 * j + half] = one_hot(recv_lo[this])
             edge[j // 4, :, place_in] = jnp.broadcast_to(recv_weight[this], (8, 128))
     lane = lanes((1, 128))
@@ -168,14 +166,15 @@
     first = (line % 2) * 128
     near, far = jnp.where(lane < 64, 127, 0), jnp.where(lane < 64, 0, 127)
     hi = jnp.broadcast_to((line // 2).astype(F32), (8, 128))
-    for p in range(32):
-        mk[32, p] = mask(hi, p)
+    hiz[...] = hi
     ohr[32] = one_hot((first + far).astype(F32))
     his[16, :, 0:128] = jnp.broadcast_to((line // 4).astype(F32), (8, 128))
     low = ((line % 4) * 128 + near).astype(F32)
     ohs[16, 0, 0:256] = one_hot(low)
     ohs[16, 0, 256:512] = one_hot(low - 256.0)
-    well = wells_ref[...]
+    tsend[0:1, 0:64] = wells_ref[...].astype(F32)
+    twice = tsend[0:1]
+    well = jnp.where(lane < 64, twice, pltpu.roll(twice, 64, 1)).astype(jnp.int32)
     well_x, well_y, well_z = well // 32768, well // 512 % 64, well % 512
     owned = (well_x // 4 == ax) & (well_y // 16 == ay) & (well_z // 128 == az)
     cell = (well_x % 4 * 16 + well_y % 16) * 128 + well_z % 128
@@ -330,7 +329,7 @@
         order = jnp.where(b == a % 16 * 16 + a // 16, 1.0, 0.0).astype(BF16)
 
         def block(i, carry):
-            k = t * 6 + i
+            k = jnp.where(t == 0, 0, t * 6 - 2) + i
             for q in range(2):
                 sides = []
                 for side in range(2):
@@ -352,7 +351,7 @@
                         )
             return carry
 
-        lax.fori_loop(0, jnp.where(t < 2, 6, 4), block, 0)
+        lax.fori_loop(0, jnp.where(t == 0, 4, 6), block, 0)
 
     def iterate(t, carry):
         now, gain = carry
@@ -364,9 +363,6 @@
             copy(here.at[pl.ds(1, 4), 16], here.at[pl.ds(1, 4), 0], hssem.at[2], hrsem.at[par, 2], up_y),
             copy(here.at[pl.ds(1, 4), 1], here.at[pl.ds(1, 4), 17], hssem.at[3], hrsem.at[par, 3], down_y),
         ]
-        for halo in halos:
-            halo.start()
-
         def stencil(r):
             x, y = 1 + r // 16, 1 + r % 16
             p, part = r // 2, slice(r % 2 * 128, r % 2 * 128 + 128)
@@ -409,12 +405,27 @@
                 copy(
                     send.at[slot], recv.at[par, slot], ssem, rsem.at[par, slot // 32], peer(SLOTS[slot])
                 ).start()
+            if group[0] == 2:
+                for halo in halos:
+                    halo.start()
         recv[par, 127] = send[127]
         for r in range(64):
             stencil(r)
         @pl.when(t == 0)
         def _():
             fetch.wait()
+
+            def build(c, carry):
+                for h in range(8):
+                    hi = hir[c, :, h * 128 : h * 128 + 128]
+                    for p in range(32):
+                        mk[8 * c + h, p] = mask(hi, p)
+                return carry
+
+            lax.fori_loop(0, 4, build, 0)
+            hi = hiz[...]
+            for p in range(32):
+                mk[32, p] = mask(hi, p)
 
         @pl.when(t < 3)
         def _():
@@ -727,6 +738,7 @@
             pltpu.VMEM((33, 256, 128), BF16),
             pltpu.VMEM((17, 8, 256), F32),
             pltpu.VMEM((4, 8, 1024), F32),
+            pltpu.VMEM((8, 128), F32),
             pltpu.VMEM((33, 32, 16, 128), BF16),
             pltpu.VMEM((128, 4, 128), F32),
             pltpu.VMEM((2, 128, 4, 128), F32),
@@ -816,7 +828,7 @@
     start_block, basis, trans_x, trans_y, trans_z, pore_volume, shift_table, shift_index,
     fault_send, fault_recv, fault_trans, well_cells,
 ):
-    wells = jnp.concatenate([well_cells, well_cells]).reshape(1, 128)
+    wells = well_cells.reshape(1, 64)
     offsets = np.zeros((8, 128), np.int32)
     offsets[0:3] = np.array(SLOTS, np.int32).T
     parts = solve(

time: 124 us -> 125 us (level)
  Pallas kernels: 122 us -> 124 us
  other arithmetic: 1.31 us -> 0 us
    pallas_call x1, Pallas kernels: 118 us -> 121 us  [solve(): pl.pallas_call(solve_kernel, out_shape=(jax.ShapeDtypeStruct((32, 32, 256...]
    reshape x1 -> x0, other arithmetic: 1.31 us -> none  [local(): wells = jnp.concatenate([well_cells, well_cells]).reshape(1, 128)]
where the time goes in v5:
time: 125 us
  Pallas kernels  124 us (99%)
  between operations  1.29 us (1%)
    pallas_call x1, Pallas kernels, solve(): pl.pallas_call(solve_kernel, out_shape=(jax.ShapeDtypeStruct((32, 32, 256...  121 us
    pallas_call x1, Pallas kernels, finish(): pl.pallas_call(finish_kernel, out_shape=(jax.ShapeDtypeStruct((1024, 128)...  3.13 us

profile of v5, /device:TPU:1, one launch (start us, length us, event | category | flops | bytes accessed | tf_op | source)
XLA Modules:
  0.0 125.3 jit_solution(966040994899808077)
XLA Ops:
  1.3 120.9 %shard_map.156 = (bf16[32,32,256]{2,1,0:T(8,128)(2,1)}, bf16[16,48]{1,0:T(8,128)(2,1)}, f32[16,256]{1,0:T(8,128)}, f32[16,256]{1,0:T(8,128)}, f32[16,64]{1,0:T(8,128)}) custom-call(f32[1024,128]{1,0:T(8,128)} %bitcast.21, bf16[16384,128]{1,0:T(8,128)(2,1)} %bitcast.20, f32[64,128]{1,0:T(8,128)} %bitcast.22, f32[64,128]{1,0:T(8,128)} %bitcast.23, ...), custom_call_target="tpu_custom_call" | custom-call | tf_op jit(solution)/shard_map/pallas_call | solution.py:720
  122.2 3.1 %shard_map.157 = (f32[1024,128]{1,0:T(8,128)}, f32[16,256]{1,0:T(8,128)}, f32[16,256]{1,0:T(8,128)}, f32[16,64]{1,0:T(8,128)}) custom-call(bf16[32,32,256]{2,1,0:T(8,128)(2,1)} %get-tuple-element.13.rest_ref, bf16[16,48]{1,0:T(8,128)(2,1)} %get-tuple-element.14.factors_ref, f32[16,256]{1,0:T(8,128)} %get-tuple-element.15.first_in, ...), custom_call_target="tpu_custom_call" | custom-call | tf_op jit(solution)/shard_map/pallas_call | solution.py:814

commit v6 on v5

--- a/solution.py
+++ b/solution.py
@@ -65,12 +65,12 @@
 
 def solve_kernel(
     start_ref, basis_ref, tx_ref, ty_ref, tz_ref, pv_ref, table_ref, index_ref, fs_ref, fr_ref, ft_ref, wells_ref, offs_ref,
-    rest, factors_ref, first_ref, coeffs_ref, resp_ref,
+    rest_ref, factors_ref, first_ref, coeffs_ref, resp_ref,
     dpad, dbf, res, xacc, acc, ohs, ohr, his, hir, hiz, mk, send, recv, zsend, zrecv, coef, edge,
-    rows, tsend, trecv, bas, bt, gmat, gfull, gsend, grecv, gall, gsum, csend, crecv, call, csum,
+    rows, tsend, trecv, bas, bt, rest, gmat, gfull, gsend, grecv, gall, gsum, csend, crecv, call, csum,
     qsend, qrecv, wsend, wrecv, wall, wsum, ohw, hiw, cmat,
     ssem, rsem, hssem, hrsem, tssem, trsem, bsem, gs1, gr1, gs2, gr2, cs1, cr1, cs2, cr2,
-    qs, qr, ws1, wr1, ws2, wr2,
+    qs, qr, ws1, wr1, ws2, wr2, ksem,
 ):
     ax, ay, az = lax.axis_index("gx"), lax.axis_index("gy"), lax.axis_index("gz")
     place = (ax, ay, az)
@@ -363,6 +363,9 @@
             copy(here.at[pl.ds(1, 4), 16], here.at[pl.ds(1, 4), 0], hssem.at[2], hrsem.at[par, 2], up_y),
             copy(here.at[pl.ds(1, 4), 1], here.at[pl.ds(1, 4), 17], hssem.at[3], hrsem.at[par, 3], down_y),
         ]
+        for halo in halos:
+            halo.start()
+
         def stencil(r):
             x, y = 1 + r // 16, 1 + r % 16
             p, part = r // 2, slice(r % 2 * 128, r % 2 * 128 + 128)
@@ -405,9 +408,6 @@
                 copy(
                     send.at[slot], recv.at[par, slot], ssem, rsem.at[par, slot // 32], peer(SLOTS[slot])
                 ).start()
-            if group[0] == 2:
-                for halo in halos:
-                    halo.start()
         recv[par, 127] = send[127]
         for r in range(64):
             stencil(r)
@@ -482,24 +482,25 @@
                 copy(gsum, gall.at[me], gs2, gr2, peer(offset)).start()
             gall[me] = gsum[...]
 
-        for halo in halos:
-            halo.wait_recv()
-
-        for y in range(16):
-            for x, which, beyond in ((0, 1, 0), (3, 0, 5)):
-                r = x * 16 + y
-                p, part = r // 2, slice(r % 2 * 128, r % 2 * 128 + 128)
-                res[p, :, part] += jnp.broadcast_to(coef[which, r : r + 1], (16, 128)) * here[beyond, 1 + y]
-        for x in range(4):
-            for y, which, beyond in ((0, 3, 0), (15, 2, 17)):
-                r = x * 16 + y
-                p, part = r // 2, slice(r % 2 * 128, r % 2 * 128 + 128)
-                res[p, :, part] += jnp.broadcast_to(coef[which, r : r + 1], (16, 128)) * here[1 + x, beyond]
         for halo in halos_z:
             halo.wait_recv()
         for side, value in enumerate(scatter(4, [half_swap(zrecv[par, 0], zrecv[par, 1])])):
             acc[side * 16 : side * 16 + 16] = value
         for j in (3, 2, 1, 0):
+            if j == 0:
+                for halo in halos:
+                    halo.wait_recv()
+
+                for y in range(16):
+                    for x, which, beyond in ((0, 1, 0), (3, 0, 5)):
+                        r = x * 16 + y
+                        p, part = r // 2, slice(r % 2 * 128, r % 2 * 128 + 128)
+                        res[p, :, part] += jnp.broadcast_to(coef[which, r : r + 1], (16, 128)) * here[beyond, 1 + y]
+                for x in range(4):
+                    for y, which, beyond in ((0, 3, 0), (15, 2, 17)):
+                        r = x * 16 + y
+                        p, part = r // 2, slice(r % 2 * 128, r % 2 * 128 + 128)
+                        res[p, :, part] += jnp.broadcast_to(coef[which, r : r + 1], (16, 128)) * here[1 + x, beyond]
             count = 32 if j < 3 else 31
             copy(
                 send.at[pl.ds(0, count)], recv.at[par, pl.ds(0, count)], ssem, rsem.at[par, j], place
@@ -639,6 +640,8 @@
         return total
 
     total = lax.fori_loop(0, 4, subtract, jnp.zeros((32, 32), F32))
+    keep = pltpu.make_async_copy(rest, rest_ref, ksem)
+    keep.start()
     gram = total[0:16, 0:16] + total[0:16, 16:32] + total[16:32, 0:16]
     lane = lanes((8, 128))
     wide = jnp.concatenate([gram, jnp.zeros((16, 112), F32)], axis=1)
@@ -690,6 +693,7 @@
     at_wells = jnp.where(lanes((16, 128)) < 64, at_wells - taken[0:16] - taken[16:32], 0.0)
     answer = jnp.dot(inverse, at_wells, precision=lax.Precision.HIGHEST, preferred_element_type=F32)
     resp_ref[...] = answer[:, 0:64]
+    keep.wait()
     exchange.wait_send()
     copy(gall.at[pl.ds(0, 127)], gall.at[pl.ds(0, 127)], gs2, gr2, place).wait_send()
     copy(qrecv.at[pl.ds(0, 127)], qrecv.at[pl.ds(0, 127)], qs, qr, place).wait_send()
@@ -727,7 +731,7 @@
             jax.ShapeDtypeStruct((16, 64), F32),
         ),
         in_specs=[vmem, pl.BlockSpec(memory_space=pl.ANY)] + [vmem] * 4 + [smem] * 2 + [vmem] * 5,
-        out_specs=(vmem,) * 5,
+        out_specs=(pl.BlockSpec(memory_space=pl.ANY),) + (vmem,) * 4,
         scratch_shapes=[
             pltpu.VMEM((2, 6, 18, 16, 128), F32),
             pltpu.VMEM((4, 256, 128), BF16),
@@ -751,6 +755,7 @@
             pltpu.VMEM((88, 128), F32),
             pltpu.VMEM((16384, 128), BF16),
             pltpu.VMEM((32, 256, 256), BF16),
+            pltpu.VMEM((32, 32, 256), BF16),
             pltpu.VMEM((4, 128, 128), F32),
             pltpu.VMEM((256, 256), F32),
             pltpu.VMEM((128, 4, 128), F32),
@@ -777,7 +782,7 @@
             dma((3,)),
             dma((3,)),
         ]
-        + [dma] * 15,
+        + [dma] * 16,
         compiler_params=pltpu.CompilerParams(
             collective_id=0, has_side_effects=True, vmem_limit_bytes=60 * 1024 * 1024
         ),

time: 125 us -> 124 us (level)
  Pallas kernels: 124 us -> 122 us
    pallas_call x1, Pallas kernels: 121 us -> 119 us  [solve(): pl.pallas_call(solve_kernel, out_shape=(jax.ShapeDtypeStruct((32, 32, 256...]
where the time goes in v6:
time: 124 us
  Pallas kernels  122 us (98%)
  between operations  1.29 us (1%)
    pallas_call x1, Pallas kernels, solve(): pl.pallas_call(solve_kernel, out_shape=(jax.ShapeDtypeStruct((32, 32, 256...  119 us
    pallas_call x1, Pallas kernels, finish(): pl.pallas_call(finish_kernel, out_shape=(jax.ShapeDtypeStruct((1024, 128)...  3.13 us

profile of v6, /device:TPU:1, one launch (start us, length us, event | category | flops | bytes accessed | tf_op | source)
XLA Modules:
  0.0 123.7 jit_solution(7141513740227754977)
XLA Ops:
  1.3 119.3 %shard_map.156 = (bf16[32,32,256]{2,1,0:T(8,128)(2,1)}, bf16[16,48]{1,0:T(8,128)(2,1)}, f32[16,256]{1,0:T(8,128)}, f32[16,256]{1,0:T(8,128)}, f32[16,64]{1,0:T(8,128)}) custom-call(f32[1024,128]{1,0:T(8,128)} %bitcast.21, bf16[16384,128]{1,0:T(8,128)(2,1)} %bitcast.20, f32[64,128]{1,0:T(8,128)} %bitcast.22, f32[64,128]{1,0:T(8,128)} %bitcast.23, ...), custom_call_target="tpu_custom_call" | custom-call | tf_op jit(solution)/shard_map/pallas_call | solution.py:724
  120.6 3.1 %shard_map.157 = (f32[1024,128]{1,0:T(8,128)}, f32[16,256]{1,0:T(8,128)}, f32[16,256]{1,0:T(8,128)}, f32[16,64]{1,0:T(8,128)}) custom-call(bf16[32,32,256]{2,1,0:T(8,128)(2,1)} %get-tuple-element.13.rest_ref, bf16[16,48]{1,0:T(8,128)(2,1)} %get-tuple-element.14.factors_ref, f32[16,256]{1,0:T(8,128)} %get-tuple-element.15.first_in, ...), custom_call_target="tpu_custom_call" | custom-call | tf_op jit(solution)/shard_map/pallas_call | solution.py:819
